TPU v7x, 256 devices: a whole 4x4x8 slice. The times are simulated.
256 devices in a mesh: pair: 32 (over z, y), red: 8 (over x, core).
Axes of the slice: x: 4, y: 4, z: 8, core: 2. Of those that a mesh axis runs over, the one named last changes fastest.
Arguments:
- amplitudes: bfloat16 [2048, 512, 640], P('pair', 'red'), may hold values from -6 to 6
- cycle_integrals: bfloat16 [640, 640], P('pair'), may hold values from -0.5 to 0.5
- ladder_integrals: bfloat16 [32, 8, 1280, 512], P('pair', 'red'), may hold values from -0.125 to 0.125
- orbital_irrep: int32 [640], replicated, may hold values from 0 to 7, as said below
- pair_irrep: int32 [2048], P('pair'), may hold values from 0 to 7, as said below
- tile_owners: int32 [8, 320], replicated, may hold values from 0 to 319, each once within a row
- ladder_tiles: int32 [32, 4], replicated, may hold values from 0 to 2559
Outputs:
- ladder_block: bfloat16 [32, 2048, 512], P('pair', 'red')
Inputs may be any that keep to these rules, and one draw needn't show every extreme that they name: Each row of tile_owners is a permutation of 0 .. 319. `orbital_irrep`: nondecreasing along the virtual orbitals; the first is 0 and the last 7. A program must be right for any labels meeting these rules, including one irrep holding nearly all orbitals. `pair_irrep`: A program must be right for any labels in the range, in any mixture.
All inputs are finite; a program needn't handle non-finite values.
Results may differ from a plain program's by a relative error of at most 0.019.
Values may be sent and summed in bfloat16 or wider, within the bound.
A program may use at most 128 MiB of HBM per device.

v0:
```python
import jax
import jax.numpy as jnp
from jax import lax
from jax.sharding import PartitionSpec as P


def irrep_lookup(irreps, indices):
    table_ids = jnp.arange(irreps.shape[0], dtype=jnp.int32)
    return jnp.sum(jnp.where(indices[..., None] == table_ids, irreps, 0), axis=-1)


def shards(
    amplitudes,
    cycle_integrals,
    ladder_integrals,
    orbital_irrep,
    pair_irrep,
    tile_owners,
    ladder_tiles,
):
    pair_count = lax.axis_size("pair")
    pair_index = lax.axis_index("pair")
    red_index = lax.axis_index("red")
    local_pairs, slab_rows, width_all = amplitudes.shape
    block_count = width_all // 128
    a_local = red_index * slab_rows + jnp.arange(slab_rows, dtype=jnp.int32)
    irrep_slab = irrep_lookup(orbital_irrep, a_local)
    allowed = (
        jnp.bitwise_xor(irrep_slab[:, None], orbital_irrep[None, :])[None]
        == pair_irrep[:, None, None]
    )
    symmetric = jnp.where(allowed, amplitudes, jnp.zeros_like(amplitudes))
    cycle_rows = cycle_integrals.shape[0]
    c_local = pair_index * cycle_rows + jnp.arange(cycle_rows, dtype=jnp.int32)
    cycle_keep = irrep_lookup(orbital_irrep, c_local)[:, None] == orbital_irrep[None, :]
    blocked = jnp.where(cycle_keep, cycle_integrals, jnp.zeros_like(cycle_integrals))
    flattened = symmetric.reshape(local_pairs * slab_rows, width_all)
    gathered_cycle = lax.all_gather(blocked, "pair", axis=0, tiled=True)
    cycle = jnp.dot(flattened, gathered_cycle, preferred_element_type=jnp.float32)
    dressed = (flattened.astype(jnp.float32) + cycle).astype(jnp.bfloat16)
    tiles_local = dressed.reshape(local_pairs, slab_rows * block_count, 128)
    slot_order = lax.dynamic_index_in_dim(tile_owners, red_index, 0, keepdims=False)
    owned_count = slot_order.shape[0] // pair_count
    ordered = jnp.take(tiles_local, slot_order, axis=1).reshape(
        local_pairs, pair_count, owned_count, 128
    )
    lane_ids = jnp.arange(128, dtype=jnp.int32)
    mine_tiles = lax.dynamic_slice_in_dim(slot_order, pair_index * owned_count, owned_count, 0)
    a_rows = red_index * slab_rows + mine_tiles // block_count
    b_cols = (mine_tiles % block_count)[:, None] * 128 + lane_ids
    irrep_cd = jnp.bitwise_xor(
        irrep_lookup(orbital_irrep, a_rows)[:, None], irrep_lookup(orbital_irrep, b_cols)
    ).reshape(-1)
    batch_ids = ladder_tiles[pair_index]
    a_out = batch_ids // block_count
    b_out = (batch_ids % block_count)[:, None] * 128 + lane_ids
    irrep_ab = jnp.bitwise_xor(
        irrep_lookup(orbital_irrep, a_out)[:, None], irrep_lookup(orbital_irrep, b_out)
    ).reshape(-1)
    weights = ladder_integrals[0, 0]
    masked = jnp.where(irrep_cd[:, None] == irrep_ab[None, :], weights, jnp.zeros_like(weights))
    total_rows = local_pairs * pair_count
    received = lax.all_to_all(ordered, "pair", split_axis=1, concat_axis=0, tiled=True)
    owned = received.reshape(total_rows, owned_count * 128)
    result = lax.psum_scatter(
        jnp.dot(owned, masked, preferred_element_type=jnp.float32).astype(jnp.bfloat16),
        "red",
        scatter_dimension=0,
        tiled=True,
    )
    return result[None]


def solution(mesh):
    return jax.shard_map(
        shards,
        mesh=mesh,
        in_specs=(
            P("pair", "red", None),
            P("pair", None),
            P("pair", "red", None, None),
            P(),
            P("pair"),
            P(),
            P(),
        ),
        out_specs=P("pair", "red", None),
        check_vma=False,
    )
```

profile of v0, /device:TPU:8, one launch (start us, length us, event | category | flops | bytes accessed | tf_op | source)
XLA Modules:
  0.0 275.5 jit_solution(3836330692513094179)
XLA Ops:
  6.5 0.7 fusion.14
  7.3 0.7 dynamic-slice_reduce_fusion
  8.0 0.9 select_reduce_fusion.2
  8.9 0.8 broadcast_xor_fusion
  9.7 0.9 select_reduce_fusion.3
  10.5 0.8 fusion.11
  11.4 53.0 %all-gather = bf16[32,20,640]{2,1,0:T(8,128)(2,1)S(1)} all-gather(bf16[1,20,640]{2,1,0:T(8,128)(2,1)S(1)} %fusion.11), channel_id=1, replica_groups=mesh['pair'=32,'red'=8] {'pair'}, dimensions={0}, use_global_device_ids=true | all-gather | bytes 844800 | tf_op jit(solution)/shard_map/all_gather | solution.py:38
  64.4 0.2 reshape.277
  64.6 4.0 %compare_select_fusion = bf16[64,64,640]{2,1,0:T(8,128)(2,1)S(1)} fusion(bf16[64,64,640]{2,1,0:T(8,128)(2,1)} %param.7, s32[64,640]{1,0:T(8,128)S(1)} %broadcast_xor_fusion, s32[64]{0:T(128)} %param.11), kind=kLoop, calls=%fused_computation.2 | loop fusion | flops 5242880 | bytes 10649856 | tf_op jit(solution)/shard_map/jit(_where)/select_n | solution.py:32
  68.6 6.8 %add_convert_fusion = bf16[4096,640]{1,0:T(8,128)(2,1)} fusion(bf16[4096,640]{1,0:T(8,128)(2,1)S(1)} %bitcast.46, bf16[640,640]{1,0:T(8,128)(2,1)S(1)} %reshape.277), kind=kOutput, calls=%fused_computation.1 | convolution fusion | flops 3363307520 | bytes 11304960 | tf_op jit(solution)/shard_map/dot_general | solution.py:39
  75.4 9.4 %reshape.266 = bf16[64,320,128]{2,1,0:T(8,128)(2,1)} reshape(bf16[4096,640]{1,0:T(8,128)(2,1)} %add_convert_fusion) | data formatting | bytes 10485760 | tf_op jit(solution)/shard_map/reshape | solution.py:41
  84.8 8.2 %copy.12 = bf16[64,320,128]{2,0,1:T(8,128)(2,1)} copy(bf16[64,320,128]{2,1,0:T(8,128)(2,1)} %reshape.266) | data formatting | bytes 10485760 | tf_op jit(solution)/shard_map/reshape | solution.py:41
  93.1 0.1 squeeze.8
  93.2 6.1 %gather_fusion = bf16[320,64,128]{2,1,0:T(8,128)(2,1)} fusion(bf16[64,320,128]{2,0,1:T(8,128)(2,1)} %copy.12, s32[1024]{0:T(1024)S(1)} %pad_clamp_fusion), kind=kCustom, calls=%fused_computation | custom fusion | bytes 10487040 | tf_op jit(solution)/shard_map/jit(_take)/gather | solution.py:44
  99.3 5.9 %broadcast_select_fusion = bf16[64,32,10,128]{3,0,2,1:T(8,128)(2,1)} fusion(bf16[64,32,10,128]{3,0,2,1:T(8,128)(2,1)} %bitcast.44, pred[32,10]{1,0:T(8,128)(4,1)S(1)} %compare_and_fusion), kind=kLoop, calls=%fused_computation.6 | loop fusion | flops 2621440 | bytes 10486080 | tf_op jit(solution)/shard_map/jit(_take)/select_n | solution.py:44
  105.3 6.8 %all-to-all-start = ((bf16[64,32,10,128]{3,0,2,1:T(8,128)(2,1)}), bf16[64,32,10,128]{3,0,2,1:T(8,128)(2,1)}, u32[]{:S(2)}, u32[]{:S(2)}) async-start(bf16[64,32,10,128]{3,0,2,1:T(8,128)(2,1)} %broadcast_select_fusion), calls=%async_computation | async-start | bytes 10485760 | tf_op jit(solution)/shard_map/all_to_all | solution.py:63
  112.1 0.2 reduce-scatter.2.cloned.1.call-start
  112.3 0.2 fusion.12
  112.5 0.2 divide_reduce_fusion
  112.7 0.8 fusion.17
  113.5 0.2 select_reduce_fusion.5
  113.7 0.2 select_reduce_fusion.4
  113.9 0.1 iota_add_fusion.1
  114.0 0.3 select_reduce_fusion.1
  114.3 0.1 iota_add_fusion
  114.3 0.6 select_reduce_fusion
  115.0 0.1 xor_bitcast_fusion.1
  115.0 0.1 xor_bitcast_fusion
  115.1 104.2 %all-to-all-done = bf16[64,32,10,128]{3,0,2,1:T(8,128)(2,1)} async-done(((bf16[64,32,10,128]{3,0,2,1:T(8,128)(2,1)}), bf16[64,32,10,128]{3,0,2,1:T(8,128)(2,1)}, u32[]{:S(2)}, u32[]{:S(2)}) %all-to-all-start) | async-done | bytes 5242912 | tf_op jit(solution)/shard_map/all_to_all | solution.py:63
  219.3 11.8 %copy.13 = bf16[32,64,1,10,128]{4,3,1,0,2:T(8,128)(2,1)S(1)} copy(bf16[32,64,1,10,128]{4,1,3,0,2:T(8,128)(2,1)} %bitcast.6) | data formatting | bytes 10485760 | tf_op jit(solution)/shard_map/all_to_all | solution.py:63
  231.1 4.4 %fusion.3 = bf16[2048,512]{1,0:T(8,128)(2,1)} fusion(bf16[256,8,10,128]{3,2,1,0:T(8,128)(2,1)S(1)} %bitcast.45, bf16[1,1,1280,512]{3,2,1,0:T(8,128)(2,1)S(1)} %copy-done.2, s32[512]{0:T(512)S(1)} %xor_bitcast_fusion.1, s32[1280]{0:T(1024)S(1)} %xor_bitcast_fusion), kind=kOutput, calls=%fused_computation.9 | convolution fusion | flops 2686713856 | bytes 8657920 | tf_op jit(solution)/shard_map/dot_general | solution.py:66
  235.5 33.2 %reduce-scatter.2.cloned.1.call-done = bf16[256,512]{1,0:T(8,128)(2,1)} async-done(((bf16[2048,512]{1,0:T(8,128)(2,1)}), bf16[256,512]{1,0:T(8,128)(2,1)}) %reduce-scatter.2.cloned.1.call-update) | async-done | bytes 262160 | tf_op jit(solution)/shard_map/reduce_scatter | solution.py:65
  (12 shorter events, 0.1 us)
Async XLA Ops:
  105.3 7.0 %copy-start.1 = (s32[32,4]{0,1:T(4,128)S(1)}, s32[32,4]{0,1:T(4,128)}, u32[]{:S(2)}) copy-start(s32[32,4]{0,1:T(4,128)} %param.13) | copy-start | bytes 1540
  105.3 8.2 %copy-start = (s32[640]{0:T(1024)S(1)}, s32[640]{0:T(1024)}, u32[]{:S(2)}) copy-start(s32[640]{0:T(1024)} %param.10) | copy-start | bytes 7684
  105.3 114.0 %all-to-all-start = ((bf16[64,32,10,128]{3,0,2,1:T(8,128)(2,1)}), bf16[64,32,10,128]{3,0,2,1:T(8,128)(2,1)}, u32[]{:S(2)}, u32[]{:S(2)}) async-start(bf16[64,32,10,128]{3,0,2,1:T(8,128)(2,1)} %broadcast_select_fusion), calls=%async_computation | async-start | bytes 10485760 | tf_op jit(solution)/shard_map/all_to_all | solution.py:63
  112.1 156.6 %reduce-scatter.2.cloned.1.call-start = ((), (), s32[]{:S(2)}) async-start(), calls=%async_computation.2 | async-start | bytes 2359296 | tf_op jit(solution)/shard_map/reduce_scatter | solution.py:65
  219.3 11.8 %copy-start.2 = (bf16[1,1,1280,512]{3,2,1,0:T(8,128)(2,1)S(1)}, bf16[1,1,1280,512]{3,2,1,0:T(8,128)(2,1)}, u32[]{:S(2)}) copy-start(bf16[1,1,1280,512]{3,2,1,0:T(8,128)(2,1)} %param.9) | copy-start | bytes 3932164
Sparse Core Ops, SparseCore 0:
  235.6 33.0 reduce-scatter.1
where the time goes:
time: 276 us
  waiting for transfers between devices  137 us (50%)
  blocking collectives  53 us (19%)
  local copies, waits for them, and re-layouts  36.6 us (13%)
  other arithmetic  16.8 us (6%)
  between operations  13.5 us (5%)
  matrix products  11.2 us (4%)
  starting transfers between devices  7.01 us (3%)
    all_to_all x1, waiting for transfers between devices, shards(): lax.all_to_all(ordered, 'pair', split_axis=1, concat_axis=0, tiled=True)  104 us
    all_gather x1, blocking collectives, shards(): gathered_cycle = lax.all_gather(blocked, 'pair', axis=0, tiled=True)  53 us
    reduce_scatter x1, waiting for transfers between devices, shards(): lax.psum_scatter(jnp.dot(owned, masked, preferred_element_type=jnp.float3...  33.2 us
    reshape x2, local copies, waits for them, and re-layouts, shards(): tiles_local = dressed.reshape(local_pairs, slab_rows * block_count, 128)  17.6 us
    all_to_all x1, local copies, waits for them, and re-layouts, shards(): lax.all_to_all(ordered, 'pair', split_axis=1, concat_axis=0, tiled=True)  11.8 us
    dot_general x1, matrix products, shards(): jnp.dot(flattened, gathered_cycle, preferred_element_type=jnp.float32)  6.8 us
    all_to_all x1, starting transfers between devices, shards(): lax.all_to_all(ordered, 'pair', split_axis=1, concat_axis=0, tiled=True)  6.79 us
    select_n x2, other arithmetic, shards(): jnp.take(tiles_local, slot_order, axis=1)  6.67 us
  transfers between devices with their start and end apart: 2, of which 2 were waited for; matrix products, arithmetic and copies ran while one was open for 1% of the time, Pallas kernels for 0%

commit v1 on v0

v1 whole, which is shorter than its diff:
```python
import jax
import jax.numpy as jnp
from jax import lax
from jax.experimental import pallas as pl
from jax.experimental.pallas import tpu as pltpu
from jax.sharding import PartitionSpec as P

NZ, NY, NR = 8, 4, 8
F32, BF16, I32 = jnp.float32, jnp.bfloat16, jnp.int32
FULL = ((0, 0), (1, 0), (-1, 0), (2, -1), (-2, 1), (2, 0), (-2, 0))
HALF = ((2, -2), (-2, 2))


def wrap(v, n):
    return lax.rem(v + n, n)


def kernel(
    amp_hbm, cyc_ref, lad_hbm, irow_ref, towners, ltiles, oirr, pirr,
    out_ref,
    amp_v, cyc_g, w_stage, w_b, irr_x, irr_c, y_stage, dressed, d_send,
    recv_f, recv_h, wbuf, ob_f, ob_h, rr_f, rr_h, fb_f, fb_h, outb,
    amp_sem, own_sem, c_send, c_recv, w_send, w_recv, a_send, a_recv,
    r_send, r_recv, f_send, f_recv,
):
    pair = lax.axis_index("pair")
    r = lax.axis_index("red")
    z, y = lax.div(pair, NY), lax.rem(pair, NY)

    def dev(zz, yy, rr):
        return (wrap(zz, NZ) * NY + wrap(yy, NY), wrap(rr, NR))

    def remote(src, dst, ssem, rsem, where):
        pltpu.make_async_remote_copy(
            src_ref=src, dst_ref=dst, send_sem=ssem, recv_sem=rsem,
            device_id=where, device_id_type=pl.DeviceIdType.MESH,
        ).start()

    def local(src, dst, sem):
        pltpu.make_async_copy(src, dst, sem).start()

    def await_bytes(ref, sem):
        pltpu.make_async_copy(ref, ref, sem).wait()

    for b in range(4):
        rows = pl.ds(b * 16, 16)
        local(amp_hbm.at[rows], amp_v.at[rows], amp_sem.at[b])
    local(lad_hbm, wbuf.at[2], own_sem)

    bar = pltpu.get_barrier_semaphore()
    me = z * NR + r

    def greet(k, _):
        i = lax.rem(me + k, NZ * NR)
        pl.semaphore_signal(
            bar, inc=1, device_id=dev(lax.div(i, NR), y, lax.rem(i, NR)),
            device_id_type=pl.DeviceIdType.MESH,
        )
        return 0

    lax.fori_loop(1, NZ * NR, greet, 0)
    for dz in range(-2, 3):
        for k in range(1, NY):
            pl.semaphore_signal(
                bar, inc=1, device_id=dev(z + dz, y + k, r),
                device_id_type=pl.DeviceIdType.MESH,
            )
    pl.semaphore_wait(bar, NZ * NR - 1 + 5 * (NY - 1))

    local(cyc_ref, cyc_g.at[y, z], c_recv.at[0])
    for k in (4, 3, 5, 2, 6, 1, 7):
        remote(cyc_ref, cyc_g.at[y, z], c_send.at[0], c_recv.at[0], dev(z + k, y, r))

    for h in range(2):
        rows = pl.ds(h * 640, 640)
        remote(lad_hbm.at[rows], wbuf.at[1, rows], w_send, w_recv.at[1, h], dev(z + 1, y, r))
        remote(lad_hbm.at[rows], wbuf.at[3, rows], w_send, w_recv.at[3, h], dev(z - 1, y, r))

    diag = lax.broadcasted_iota(I32, (128, 128), 0) == lax.broadcasted_iota(I32, (128, 128), 1)
    for k in range(5):
        lab = jnp.broadcast_to(irow_ref[:, k * 128 : (k + 1) * 128], (128, 128))
        col = jnp.sum(jnp.where(diag, lab, 0), axis=1, keepdims=True)
        irr_c[k * 128 : (k + 1) * 128, :] = jnp.broadcast_to(col, (128, 128))
    slab = irr_c[pl.ds(pl.multiple_of(r * 64, 64), 64), :]
    for k in range(5):
        irr_x[:, k * 128 : (k + 1) * 128] = jnp.bitwise_xor(slab, irow_ref[:, k * 128 : (k + 1) * 128])

    await_bytes(cyc_g.at[y], c_recv.at[0])
    for k in (2, 1, 3):
        remote(cyc_g.at[y], cyc_g.at[y], c_send.at[1], c_recv.at[1], dev(z, y + k, r))
    await_bytes(cyc_g.at[pl.ds(0, NY - 1)], c_recv.at[1])

    def forward(h):
        rows = pl.ds(h * 640, 640)
        for a, b, dz in ((1, 0, 1), (3, 4, -1)):
            await_bytes(wbuf.at[a, rows], w_recv.at[a, h])
            remote(wbuf.at[a, rows], wbuf.at[b, rows], w_send, w_recv.at[b, h], dev(z + dz, y, r))

    for p in range(NZ * NY):
        w_stage[p * 20 : p * 20 + 20, :] = cyc_g[p % NY, p // NY][:20, :].astype(F32)

    def mask_w(c, _):
        rows = pl.ds(pl.multiple_of(c * 128, 128), 128)
        for k in range(5):
            cols = slice(k * 128, (k + 1) * 128)
            keep = irr_c[rows, :] == irow_ref[:, cols]
            w_b[rows, cols] = jnp.where(keep, w_stage[rows, cols], 0.0).astype(BF16)
        return 0

    lax.fori_loop(0, 5, mask_w, 0)

    def dress(b, _):
        await_bytes(amp_v.at[pl.ds(0, 16)], amp_sem.at[b])

        def quad(q, _):
            ij = b * 16 + q * 4
            x = amp_v[pl.ds(ij, 4)].reshape(256, 640)
            v = jnp.dot(x, w_b[...], preferred_element_type=F32) + x.astype(F32)
            for e in range(4):
                label = pirr[ij + e]
                at = pl.ds(pl.multiple_of((q * 4 + e) * 64, 64), 64)
                for k in range(5):
                    cols = slice(k * 128, (k + 1) * 128)
                    y_stage[k, at, :] = jnp.where(irr_x[:, cols] == label, v[e * 64 : (e + 1) * 64, cols], 0.0)
            return 0

        lax.fori_loop(0, 4, quad, 0)

        def turn(a, _):
            for k in range(5):
                v = y_stage[k, pl.ds(a, 16, stride=64), :]
                dressed[a * 5 + k, pl.ds(pl.multiple_of(b * 16, 16), 16), :] = v.astype(BF16)
            return 0

        lax.fori_loop(0, 64, turn, 0)
        return 0

    lax.fori_loop(0, 4, dress, 0)
    forward(0)

    def order(delta):
        def one(yy, _):
            first = (wrap(z + delta, NZ) * NY + yy) * 10
            for s in range(10):
                d_send[delta % 8, yy, :, s * 128 : (s + 1) * 128] = dressed[towners[r, first + s]]
            return 0

        lax.fori_loop(0, NY, one, 0)

    mine = pl.ds(pl.multiple_of(y * 64, 64), 64)
    mine_h = pl.ds(pl.multiple_of(y * 32, 32), 32)
    for slot, delta, dz in ((0, 0, 0), (1, 1, 0), (2, -1, 0), (3, 3, 1), (4, -3, -1), (None, 4, 2), (5, 2, 0), (6, -2, 0)):
        order(delta)
        buf = d_send.at[delta % 8]
        if slot is None:
            for k in (2, 1, 3, 0):
                yy = wrap(y + k, NY)
                remote(buf.at[yy, pl.ds(0, 32)], recv_h.at[0, mine_h], a_send, a_recv.at[7], dev(z + 2, yy, r))
                remote(buf.at[yy, pl.ds(32, 32)], recv_h.at[1, mine_h], a_send, a_recv.at[8], dev(z - 2, yy, r))
            continue
        for k in (2, 1, 3, 0):
            yy = wrap(y + k, NY)
            if dz == 0 and k == 0:
                local(buf.at[yy], recv_f.at[slot, mine], a_recv.at[slot])
            else:
                remote(buf.at[yy], recv_f.at[slot, mine], a_send, a_recv.at[slot], dev(z + dz, yy, r))
    forward(1)

    def multiply(x, w, o):
        def cols(n, _):
            at = pl.ds(pl.multiple_of(n * 256, 256), 256)
            o[:, at] = jnp.dot(x[...], w[:, at], preferred_element_type=F32).astype(BF16)
            return 0

        lax.fori_loop(0, 2, cols, 0)

    def scatter(o, rr, n, sem):
        def piece(q):
            return o.at[pl.ds(pl.multiple_of(q * n, n), n)]

        for k in (4, 3, 5, 2, 6, 1, 7):
            q = wrap(r + k, NR)
            remote(piece(q), rr.at[r], r_send, sem, dev(z, y, q))
        local(piece(r), rr.at[r], sem)

    def reduce(item):
        if item < 7:
            (o, s), rr, fb, n = FULL[item], rr_f.at[item], fb_f.at[item], 32
            row = r * 32
        else:
            (o, s), rr, fb, n = HALF[item - 7], rr_h.at[item - 7], fb_h.at[item - 7], 16
            row = lax.div(r, 2) * 64 + lax.rem(r, 2) * 16 + (item - 7) * 32
        await_bytes(rr, r_recv.at[item])
        total = rr[0].astype(F32)
        for q in range(1, NR):
            total = total + rr[q].astype(F32)
        fb[...] = total.astype(BF16)
        rows = outb.at[pl.ds(pl.multiple_of(row, 16), n)]
        level = wrap(z + s, NZ)
        if item == 0:

            @pl.when(level == r)
            def _():
                local(fb, rows, f_recv)

            @pl.when(level != r)
            def _():
                remote(fb, rows, f_send.at[0], f_recv, dev(z + o, y, level))
        else:
            remote(fb, rows, f_send.at[1], f_recv, dev(z + o, y, level))

    ready = {2}

    def item_step(item):
        if item < 7:
            o, x, ob, rr, n = FULL[item][0], recv_f.at[item], ob_f.at[item], rr_f.at[item], 32
        else:
            o, x, ob, rr, n = HALF[item - 7][0], recv_h.at[item - 7], ob_h.at[item - 7], rr_h.at[item - 7], 16
        if item == 0:
            await_bytes(wbuf.at[2], own_sem)
        if o in (2, -2) and o + 2 not in ready:
            ready.add(o + 2)
            for h in range(2):
                await_bytes(wbuf.at[o + 2, pl.ds(h * 640, 640)], w_recv.at[o + 2, h])
        await_bytes(x, a_recv.at[item])
        multiply(x, wbuf.at[o + 2], ob)
        scatter(ob, rr, n, r_recv.at[item])

    todo = (0, 1, 2, 3, 4, 7, 8, 5, 6)
    for at, item in enumerate(todo):
        item_step(item)
        if at:
            reduce(todo[at - 1])
    reduce(todo[-1])

    diag64 = lax.broadcasted_iota(I32, (64, 128), 0) == lax.broadcasted_iota(I32, (64, 128), 1)
    await_bytes(outb, f_recv)
    for j in range(4):
        t = ltiles[pair, j]
        la, bb = oirr[lax.div(t, 5)], lax.rem(t, 5)
        lab = jnp.zeros((1, 128), I32)
        for k in range(5):
            lab = lab + jnp.where(bb == k, irow_ref[:, k * 128 : (k + 1) * 128], 0)
        lab = jnp.bitwise_xor(lab, la).astype(F32)
        for yy in range(NY):
            rowl = cyc_g[yy, r][20:21, 0:128].astype(F32)
            col = jnp.sum(jnp.where(diag64, jnp.broadcast_to(rowl, (64, 128)), 0.0), axis=1, keepdims=True)
            keep = jnp.broadcast_to(col, (64, 128)) == lab
            got = outb[yy * 64 : (yy + 1) * 64, j * 128 : (j + 1) * 128].astype(F32)
            out_ref[yy * 64 : (yy + 1) * 64, j * 128 : (j + 1) * 128] = jnp.where(keep, got, 0.0).astype(BF16)

    await_bytes(cyc_g.at[0, pl.ds(0, NZ - 1)], c_send.at[0])
    await_bytes(cyc_g.at[pl.ds(0, NY - 1)], c_send.at[1])
    await_bytes(wbuf.at[pl.ds(0, 4)], w_send)
    await_bytes(d_send.at[pl.ds(0, 6)], a_send)
    await_bytes(d_send.at[0, pl.ds(0, 3)], a_send)
    await_bytes(rr_f.at[:, pl.ds(0, NR - 1)], r_send)
    await_bytes(rr_h.at[:, pl.ds(0, NR - 1)], r_send)

    @pl.when(z != r)
    def _():
        await_bytes(fb_f.at[0], f_send.at[0])

    await_bytes(fb_f.at[pl.ds(0, 6)], f_send.at[1])
    await_bytes(fb_h, f_send.at[1])


def shards(amplitudes, cycle_integrals, ladder_integrals, orbital_irrep, pair_irrep, tile_owners, ladder_tiles):
    cyc = jnp.zeros((24, 640), BF16)
    cyc = cyc.at[:20].set(cycle_integrals).at[20, :64].set(pair_irrep.astype(BF16))
    hbm = pl.BlockSpec(memory_space=pltpu.MemorySpace.HBM)
    vmem = pl.BlockSpec(memory_space=pltpu.MemorySpace.VMEM)
    smem = pl.BlockSpec(memory_space=pltpu.MemorySpace.SMEM)
    dma = pltpu.SemaphoreType.DMA
    out = pl.pallas_call(
        kernel,
        out_shape=jax.ShapeDtypeStruct((256, 512), BF16),
        in_specs=[hbm, vmem, hbm, vmem, smem, smem, smem, smem],
        out_specs=vmem,
        scratch_shapes=[
            pltpu.VMEM((64, 64, 640), BF16),
            pltpu.VMEM((4, 8, 24, 640), BF16),
            pltpu.VMEM((640, 640), F32),
            pltpu.VMEM((640, 640), BF16),
            pltpu.VMEM((64, 640), I32),
            pltpu.VMEM((640, 128), I32),
            pltpu.VMEM((5, 1024, 128), F32),
            pltpu.VMEM((320, 64, 128), BF16),
            pltpu.VMEM((8, 4, 64, 1280), BF16),
            pltpu.VMEM((7, 256, 1280), BF16),
            pltpu.VMEM((2, 128, 1280), BF16),
            pltpu.VMEM((5, 1280, 512), BF16),
            pltpu.VMEM((7, 256, 512), BF16),
            pltpu.VMEM((2, 128, 512), BF16),
            pltpu.VMEM((7, 8, 32, 512), BF16),
            pltpu.VMEM((2, 8, 16, 512), BF16),
            pltpu.VMEM((7, 32, 512), BF16),
            pltpu.VMEM((2, 16, 512), BF16),
            pltpu.VMEM((256, 512), BF16),
            dma((4,)),
            dma,
            dma((2,)),
            dma((2,)),
            dma,
            dma((5, 2)),
            dma,
            dma((9,)),
            dma,
            dma((9,)),
            dma((2,)),
            dma,
        ],
        compiler_params=pltpu.CompilerParams(
            collective_id=0, has_side_effects=True, vmem_limit_bytes=56 << 20
        ),
        name="ladder",
    )(
        amplitudes,
        cyc,
        ladder_integrals.reshape(1280, 512),
        orbital_irrep.reshape(1, 640),
        tile_owners,
        ladder_tiles,
        orbital_irrep,
        pair_irrep,
    )
    return out[None]


def solution(mesh):
    return jax.shard_map(
        shards,
        mesh=mesh,
        in_specs=(
            P("pair", "red", None),
            P("pair", None),
            P("pair", "red", None, None),
            P(),
            P("pair"),
            P(),
            P(),
        ),
        out_specs=P("pair", "red", None),
        check_vma=False,
    )
```

time: 276 us -> 156 us (0.57)
  the two profiles are of different devices: /device:TPU:8 before, /device:TPU:4 now
where the time goes in v1:
time: 156 us; the launch traced here: 153 us
  Pallas kernels  147 us (94%)
  local copies, waits for them, and re-layouts  5.77 us (4%)
    pallas_call x1, Pallas kernels, shards(): pl.pallas_call(kernel, out_shape=jax.ShapeDtypeStruct((256, 512), BF16),...  147 us
    unnamed x4, local copies, waits for them, and re-layouts  3.63 us

profile of v1, /device:TPU:4, one launch (start us, length us, event | category | flops | bytes accessed | tf_op | source)
XLA Modules:
  0.0 153.2 jit_solution(16933389730625901788)
XLA Ops:
  0.0 0.7 convert_bitcast_fusion
  0.7 1.3 reshape.64.irow_ref
  1.9 1.4 copy.8.ltiles
  3.3 0.8 scatter.6
  4.1 0.1 scatter.9.cyc_ref
  4.2 0.0 copy-start
  4.2 0.6 copy-done
  4.8 146.8 %ladder.1 = bf16[256,512]{1,0:T(8,128)(2,1)} custom-call(bf16[64,64,640]{2,1,0:T(8,128)(2,1)} %amp_hbm.1, bf16[24,640]{1,0:T(8,128)(2,1)} %copy-done, bf16[1280,512]{1,0:T(8,128)(2,1)} %bitcast.4, s32[1,640]{1,0:T(1,128)} %reshape.64.irow_ref, s32[8,320]{1,0:T(8,128)} %towners.1, s32[32,4]{1,0:T(8,128)} %copy.8.ltiles, s32[640]{0:T(1024)} %oirr.1, s32[64]{0:T(128)} %pirr.1), custom_call_target="tpu_custom_call" | custom-call | tf_op jit(solution)/shard_map/ladder/pallas_call | solution.py:275
  151.5 1.7 %copy.11 = bf16[1,256,512]{2,1,0:T(8,128)(2,1)} copy(bf16[1,256,512]{2,1,0:T(8,128)(2,1)} %bitcast.5) | data formatting | bytes 524288
Async XLA Ops:
  4.2 0.6 copy-start

commit v2 on v1

--- a/solution.py
+++ b/solution.py
@@ -9,6 +9,11 @@
 F32, BF16, I32 = jnp.float32, jnp.bfloat16, jnp.int32
 FULL = ((0, 0), (1, 0), (-1, 0), (2, -1), (-2, 1), (2, 0), (-2, 0))
 HALF = ((2, -2), (-2, 2))
+WAY = (0, 3, -3, 4, 1, -1, 2, -2)
+NEAR = {0: 0, 1: 1, -1: 2, 2: 5, -2: 6}
+FAR = {3: 0, -3: 1, 4: 2}
+TODO = {0: (0,), 1: (1,), -1: (2,), 2: (3, 4, 5), -2: (6, 7, 8)}
+WINDOW = 3
 
 
 def wrap(v, n):
@@ -16,12 +21,12 @@
 
 
 def kernel(
-    amp_hbm, cyc_ref, lad_hbm, irow_ref, towners, ltiles, oirr, pirr,
+    amp_hbm, cyc_ref, lad_hbm, towners, ltiles, oirr, pirr,
     out_ref,
-    amp_v, cyc_g, w_stage, w_b, irr_x, irr_c, y_stage, dressed, d_send,
-    recv_f, recv_h, wbuf, ob_f, ob_h, rr_f, rr_h, fb_f, fb_h, outb,
+    amp_v, cyc_g, w_stage, w_b, irow_ref, irr_x, irr_c, y_stage, dressed, d_send,
+    recv_f, recv_h, far, wbuf, ob_f, ob_h, rr_f, rr_h, fb_f, fb_h, outb,
     amp_sem, own_sem, c_send, c_recv, w_send, w_recv, a_send, a_recv,
-    r_send, r_recv, f_send, f_recv,
+    x_send, x_recv, r_send, r_recv, f_send, f_recv,
 ):
     pair = lax.axis_index("pair")
     r = lax.axis_index("red")
@@ -59,23 +64,12 @@
         return 0
 
     lax.fori_loop(1, NZ * NR, greet, 0)
-    for dz in range(-2, 3):
-        for k in range(1, NY):
-            pl.semaphore_signal(
-                bar, inc=1, device_id=dev(z + dz, y + k, r),
-                device_id_type=pl.DeviceIdType.MESH,
-            )
-    pl.semaphore_wait(bar, NZ * NR - 1 + 5 * (NY - 1))
-
-    local(cyc_ref, cyc_g.at[y, z], c_recv.at[0])
-    for k in (4, 3, 5, 2, 6, 1, 7):
-        remote(cyc_ref, cyc_g.at[y, z], c_send.at[0], c_recv.at[0], dev(z + k, y, r))
-
-    for h in range(2):
-        rows = pl.ds(h * 640, 640)
-        remote(lad_hbm.at[rows], wbuf.at[1, rows], w_send, w_recv.at[1, h], dev(z + 1, y, r))
-        remote(lad_hbm.at[rows], wbuf.at[3, rows], w_send, w_recv.at[3, h], dev(z - 1, y, r))
-
+    for k in range(1, NY):
+        pl.semaphore_signal(
+            bar, inc=1, device_id=dev(z, y + k, r),
+            device_id_type=pl.DeviceIdType.MESH,
+        )
+    irow_ref[...] = cyc_ref[21:22, :].astype(F32).astype(I32)
     diag = lax.broadcasted_iota(I32, (128, 128), 0) == lax.broadcasted_iota(I32, (128, 128), 1)
     for k in range(5):
         lab = jnp.broadcast_to(irow_ref[:, k * 128 : (k + 1) * 128], (128, 128))
@@ -85,10 +79,31 @@
     for k in range(5):
         irr_x[:, k * 128 : (k + 1) * 128] = jnp.bitwise_xor(slab, irow_ref[:, k * 128 : (k + 1) * 128])
 
-    await_bytes(cyc_g.at[y], c_recv.at[0])
+    pl.semaphore_wait(bar, NZ * NR - 1 + NY - 1)
+
+    core = lax.rem(r, 2)
+    sends = lax.rem(z, 2) == core
+
+    @pl.when(sends)
+    def _():
+        to = cyc_g.at[y, core, lax.div(z, 2)]
+        local(cyc_ref, to, c_recv.at[0])
+        for k in (4, 3, 5, 2, 6, 1, 7):
+            remote(cyc_ref, to, c_send.at[0], c_recv.at[0], dev(z + k, y, r))
+
+    for h in range(2):
+        rows = pl.ds(h * 640, 640)
+        remote(lad_hbm.at[rows], wbuf.at[1, rows], w_send, w_recv.at[1, h], dev(z + 1, y, r))
+        remote(lad_hbm.at[rows], wbuf.at[3, rows], w_send, w_recv.at[3, h], dev(z - 1, y, r))
+
+    part = cyc_g.at[y, core]
+    await_bytes(part, c_recv.at[0])
     for k in (2, 1, 3):
-        remote(cyc_g.at[y], cyc_g.at[y], c_send.at[1], c_recv.at[1], dev(z, y + k, r))
-    await_bytes(cyc_g.at[pl.ds(0, NY - 1)], c_recv.at[1])
+        remote(part, part, c_send.at[1], c_recv.at[1], dev(z, y + k, r))
+    await_bytes(cyc_g.at[pl.ds(0, NY - 1), 0], c_recv.at[1])
+    part = cyc_g.at[:, core]
+    remote(part, part, c_send.at[2], c_recv.at[2], dev(z, y, r + 1 - 2 * core))
+    await_bytes(part, c_recv.at[2])
 
     def forward(h):
         rows = pl.ds(h * 640, 640)
@@ -97,7 +112,7 @@
             remote(wbuf.at[a, rows], wbuf.at[b, rows], w_send, w_recv.at[b, h], dev(z + dz, y, r))
 
     for p in range(NZ * NY):
-        w_stage[p * 20 : p * 20 + 20, :] = cyc_g[p % NY, p // NY][:20, :].astype(F32)
+        w_stage[p * 20 : p * 20 + 20, :] = cyc_g[p % NY, (p // NY) % 2, p // NY // 2][:20, :].astype(F32)
 
     def mask_w(c, _):
         rows = pl.ds(pl.multiple_of(c * 128, 128), 128)
@@ -126,17 +141,19 @@
 
         lax.fori_loop(0, 4, quad, 0)
 
-        def turn(a, _):
-            for k in range(5):
-                v = y_stage[k, pl.ds(a, 16, stride=64), :]
-                dressed[a * 5 + k, pl.ds(pl.multiple_of(b * 16, 16), 16), :] = v.astype(BF16)
+        def turn(c, _):
+            at = pl.ds(pl.multiple_of(b * 16, 16), 16)
+            got = [y_stage[k, pl.ds(c * 8 + i, 16, stride=64), :].astype(BF16) for i in range(8) for k in range(5)]
+            for i in range(40):
+                dressed[c * 40 + i, at, :] = got[i]
             return 0
 
-        lax.fori_loop(0, 64, turn, 0)
+        lax.fori_loop(0, 8, turn, 0)
         return 0
 
-    lax.fori_loop(0, 4, dress, 0)
+    lax.fori_loop(0, 2, dress, 0)
     forward(0)
+    lax.fori_loop(2, 4, dress, 0)
 
     def order(delta):
         def one(yy, _):
@@ -148,22 +165,33 @@
         lax.fori_loop(0, NY, one, 0)
 
     mine = pl.ds(pl.multiple_of(y * 64, 64), 64)
-    mine_h = pl.ds(pl.multiple_of(y * 32, 32), 32)
-    for slot, delta, dz in ((0, 0, 0), (1, 1, 0), (2, -1, 0), (3, 3, 1), (4, -3, -1), (None, 4, 2), (5, 2, 0), (6, -2, 0)):
+
+    def send(delta):
         order(delta)
         buf = d_send.at[delta % 8]
-        if slot is None:
-            for k in (2, 1, 3, 0):
-                yy = wrap(y + k, NY)
-                remote(buf.at[yy, pl.ds(0, 32)], recv_h.at[0, mine_h], a_send, a_recv.at[7], dev(z + 2, yy, r))
-                remote(buf.at[yy, pl.ds(32, 32)], recv_h.at[1, mine_h], a_send, a_recv.at[8], dev(z - 2, yy, r))
-            continue
-        for k in (2, 1, 3, 0):
+        if delta in FAR:
+            to, sem = far.at[FAR[delta], mine], x_recv.at[FAR[delta]]
+        else:
+            to, sem = recv_f.at[NEAR[delta], mine], a_recv.at[NEAR[delta]]
+        local(buf.at[y], to, sem)
+        for k in (2, 1, 3):
             yy = wrap(y + k, NY)
-            if dz == 0 and k == 0:
-                local(buf.at[yy], recv_f.at[slot, mine], a_recv.at[slot])
-            else:
-                remote(buf.at[yy], recv_f.at[slot, mine], a_send, a_recv.at[slot], dev(z + dz, yy, r))
+            remote(buf.at[yy], to, a_send.at[delta % 8], sem, dev(z, yy, r))
+
+    def sent(delta):
+        await_bytes(d_send.at[0, pl.ds(0, NY - 1)], a_send.at[delta % 8])
+
+    def go_on(delta):
+        at = FAR[delta]
+        await_bytes(far.at[at], x_recv.at[at])
+        if delta == 4:
+            remote(far.at[at, pl.ds(0, 128)], recv_h.at[0], x_send, a_recv.at[7], dev(z + 2, y, r))
+            remote(far.at[at, pl.ds(128, 128)], recv_h.at[1], x_send, a_recv.at[8], dev(z - 2, y, r))
+        else:
+            remote(far.at[at], recv_f.at[3 + at], x_send, a_recv.at[3 + at], dev(z + 1 - 2 * at, y, r))
+
+    for delta in WAY[:WINDOW]:
+        send(delta)
     forward(1)
 
     def multiply(x, w, o):
@@ -189,7 +217,7 @@
             row = r * 32
         else:
             (o, s), rr, fb, n = HALF[item - 7], rr_h.at[item - 7], fb_h.at[item - 7], 16
-            row = lax.div(r, 2) * 64 + lax.rem(r, 2) * 16 + (item - 7) * 32
+            row = r * 16 + (item - 7) * 128
         await_bytes(rr, r_recv.at[item])
         total = rr[0].astype(F32)
         for q in range(1, NR):
@@ -226,34 +254,48 @@
         multiply(x, wbuf.at[o + 2], ob)
         scatter(ob, rr, n, r_recv.at[item])
 
-    todo = (0, 1, 2, 3, 4, 7, 8, 5, 6)
-    for at, item in enumerate(todo):
-        item_step(item)
-        if at:
-            reduce(todo[at - 1])
-    reduce(todo[-1])
+    last = None
+    for i, delta in enumerate(WAY):
+        if i + WINDOW < 8:
+            sent(delta)
+            send(WAY[i + WINDOW])
+        if delta in FAR:
+            go_on(delta)
+            continue
+        for item in TODO[delta]:
+            item_step(item)
+            if last is not None:
+                reduce(last)
+            last = item
+    reduce(last)
 
     diag64 = lax.broadcasted_iota(I32, (64, 128), 0) == lax.broadcasted_iota(I32, (64, 128), 1)
     await_bytes(outb, f_recv)
     for j in range(4):
-        t = ltiles[pair, j]
+        t = ltiles[j, pair]
         la, bb = oirr[lax.div(t, 5)], lax.rem(t, 5)
         lab = jnp.zeros((1, 128), I32)
         for k in range(5):
             lab = lab + jnp.where(bb == k, irow_ref[:, k * 128 : (k + 1) * 128], 0)
         lab = jnp.bitwise_xor(lab, la).astype(F32)
         for yy in range(NY):
-            rowl = cyc_g[yy, r][20:21, 0:128].astype(F32)
+            rowl = cyc_g[yy, core, lax.div(r, 2)][20:21, 0:128].astype(F32)
             col = jnp.sum(jnp.where(diag64, jnp.broadcast_to(rowl, (64, 128)), 0.0), axis=1, keepdims=True)
             keep = jnp.broadcast_to(col, (64, 128)) == lab
             got = outb[yy * 64 : (yy + 1) * 64, j * 128 : (j + 1) * 128].astype(F32)
             out_ref[yy * 64 : (yy + 1) * 64, j * 128 : (j + 1) * 128] = jnp.where(keep, got, 0.0).astype(BF16)
 
-    await_bytes(cyc_g.at[0, pl.ds(0, NZ - 1)], c_send.at[0])
-    await_bytes(cyc_g.at[pl.ds(0, NY - 1)], c_send.at[1])
+    @pl.when(sends)
+    def _():
+        await_bytes(cyc_g.at[0, 0], c_send.at[0])
+        await_bytes(cyc_g.at[0, 1, pl.ds(0, 3)], c_send.at[0])
+
+    await_bytes(cyc_g.at[pl.ds(0, NY - 1), 0], c_send.at[1])
+    await_bytes(cyc_g.at[:, 0], c_send.at[2])
     await_bytes(wbuf.at[pl.ds(0, 4)], w_send)
-    await_bytes(d_send.at[pl.ds(0, 6)], a_send)
-    await_bytes(d_send.at[0, pl.ds(0, 3)], a_send)
+    for delta in WAY[8 - WINDOW :]:
+        sent(delta)
+    await_bytes(far, x_send)
     await_bytes(rr_f.at[:, pl.ds(0, NR - 1)], r_send)
     await_bytes(rr_h.at[:, pl.ds(0, NR - 1)], r_send)
 
@@ -266,8 +308,11 @@
 
 
 def shards(amplitudes, cycle_integrals, ladder_integrals, orbital_irrep, pair_irrep, tile_owners, ladder_tiles):
-    cyc = jnp.zeros((24, 640), BF16)
-    cyc = cyc.at[:20].set(cycle_integrals).at[20, :64].set(pair_irrep.astype(BF16))
+    row = lax.broadcasted_iota(I32, (24, 640), 0)
+    cyc = jnp.where(row < 20, jnp.pad(cycle_integrals, ((0, 4), (0, 0))), jnp.zeros((), BF16))
+    labels = jnp.pad(pair_irrep, (0, 576))[None, :].astype(BF16)
+    cyc = jnp.where(row == 20, labels, cyc)
+    cyc = jnp.where(row == 21, orbital_irrep[None, :].astype(BF16), cyc)
     hbm = pl.BlockSpec(memory_space=pltpu.MemorySpace.HBM)
     vmem = pl.BlockSpec(memory_space=pltpu.MemorySpace.VMEM)
     smem = pl.BlockSpec(memory_space=pltpu.MemorySpace.SMEM)
@@ -275,13 +320,14 @@
     out = pl.pallas_call(
         kernel,
         out_shape=jax.ShapeDtypeStruct((256, 512), BF16),
-        in_specs=[hbm, vmem, hbm, vmem, smem, smem, smem, smem],
+        in_specs=[hbm, vmem, hbm, smem, smem, smem, smem],
         out_specs=vmem,
         scratch_shapes=[
             pltpu.VMEM((64, 64, 640), BF16),
-            pltpu.VMEM((4, 8, 24, 640), BF16),
+            pltpu.VMEM((4, 2, 4, 24, 640), BF16),
             pltpu.VMEM((640, 640), F32),
             pltpu.VMEM((640, 640), BF16),
+            pltpu.VMEM((1, 640), I32),
             pltpu.VMEM((64, 640), I32),
             pltpu.VMEM((640, 128), I32),
             pltpu.VMEM((5, 1024, 128), F32),
@@ -289,6 +335,7 @@
             pltpu.VMEM((8, 4, 64, 1280), BF16),
             pltpu.VMEM((7, 256, 1280), BF16),
             pltpu.VMEM((2, 128, 1280), BF16),
+            pltpu.VMEM((3, 256, 1280), BF16),
             pltpu.VMEM((5, 1280, 512), BF16),
             pltpu.VMEM((7, 256, 512), BF16),
             pltpu.VMEM((2, 128, 512), BF16),
@@ -299,12 +346,14 @@
             pltpu.VMEM((256, 512), BF16),
             dma((4,)),
             dma,
-            dma((2,)),
-            dma((2,)),
+            dma((3,)),
+            dma((3,)),
             dma,
             dma((5, 2)),
-            dma,
+            dma((8,)),
             dma((9,)),
+            dma,
+            dma((3,)),
             dma,
             dma((9,)),
             dma((2,)),
@@ -318,9 +367,8 @@
         amplitudes,
         cyc,
         ladder_integrals.reshape(1280, 512),
-        orbital_irrep.reshape(1, 640),
         tile_owners,
-        ladder_tiles,
+        ladder_tiles.T,
         orbital_irrep,
         pair_irrep,
     )

time: 156 us -> 122 us (0.78); the launches traced: 153 us -> 121 us
  Pallas kernels: 147 us -> 117 us
  local copies, waits for them, and re-layouts: 5.77 us -> 1.67 us
  other arithmetic: 0.66 us -> 2.8 us
    pallas_call x1, Pallas kernels: 147 us -> 117 us  [shards(): pl.pallas_call(kernel, out_shape=jax.ShapeDtypeStruct((256, 512), BF16),...]
    unnamed x4 -> x1, local copies, waits for them, and re-layouts: 3.63 us -> 1.67 us
where the time goes in v2:
time: 122 us; the launch traced here: 121 us
  Pallas kernels  117 us (96%)
  other arithmetic  2.8 us (2%)
  local copies, waits for them, and re-layouts  1.67 us (1%)
    pallas_call x1, Pallas kernels, shards(): pl.pallas_call(kernel, out_shape=jax.ShapeDtypeStruct((256, 512), BF16),...  117 us

profile of v2, /device:TPU:4, one launch (start us, length us, event | category | flops | bytes accessed | tf_op | source)
XLA Modules:
  0.0 121.3 jit_solution(4393726072671627001)
XLA Ops:
  0.0 0.7 convert.4
  0.7 0.7 convert_element_type.8
  1.4 1.4 %select_select_fusion.cyc_ref = bf16[24,640]{1,0:T(8,128)(2,1)} fusion(bf16[20,640]{1,0:T(8,128)(2,1)} %param.8, pred[24]{0:T(512)(128)(4,1)S(1)} %get-tuple-element.5, pred[24]{0:T(512)(128)(4,1)S(1)} %get-tuple-element.6, pred[24]{0:T(512)(128)(4,1)S(1)} %iota_compare_fusion.2, bf16[640]{0:T(1024)(128)(2,1)S(1)} %pad.9, bf16[640]{0:T(1024)(128)(2,1)S(1)} %convert_element_type.8), kind=kLoop, calls=%fused_computation | loop fusion | flops 46080 | bytes 58952 | tf_op jit(solution)/shard_map/jit(_where)/select_n | solution.py:315
  2.8 116.8 %ladder.1 = bf16[256,512]{1,0:T(8,128)(2,1)} custom-call(bf16[64,64,640]{2,1,0:T(8,128)(2,1)} %amp_hbm.1, bf16[24,640]{1,0:T(8,128)(2,1)} %select_select_fusion.cyc_ref, bf16[1280,512]{1,0:T(8,128)(2,1)} %bitcast.3, s32[8,320]{1,0:T(8,128)} %towners.1, s32[4,32]{1,0:T(4,128)} %bitcast.5, s32[640]{0:T(1024)} %oirr.1, s32[64]{0:T(128)} %pirr.1), custom_call_target="tpu_custom_call" | custom-call | tf_op jit(solution)/shard_map/ladder/pallas_call | solution.py:320
  119.6 1.7 %copy.9 = bf16[1,256,512]{2,1,0:T(8,128)(2,1)} copy(bf16[1,256,512]{2,1,0:T(8,128)(2,1)} %bitcast.4) | data formatting | bytes 524288
  (3 shorter events, 0.0 us)

commit v3 on v2

--- a/solution.py
+++ b/solution.py
@@ -21,9 +21,9 @@
 
 
 def kernel(
-    amp_hbm, cyc_ref, lad_hbm, towners, ltiles, oirr, pirr,
+    amp_hbm, cyc_in, lad_hbm, orow, prow, towners, ltiles, oirr, pirr,
     out_ref,
-    amp_v, cyc_g, w_stage, w_b, irow_ref, irr_x, irr_c, y_stage, dressed, d_send,
+    amp_v, cyc_ref, cyc_g, w_stage, w_b, irow_ref, irr_x, irr_c, y_stage, dressed, d_send,
     recv_f, recv_h, far, wbuf, ob_f, ob_h, rr_f, rr_h, fb_f, fb_h, outb,
     amp_sem, own_sem, c_send, c_recv, w_send, w_recv, a_send, a_recv,
     x_send, x_recv, r_send, r_recv, f_send, f_recv,
@@ -69,7 +69,11 @@
             bar, inc=1, device_id=dev(z, y + k, r),
             device_id_type=pl.DeviceIdType.MESH,
         )
-    irow_ref[...] = cyc_ref[21:22, :].astype(F32).astype(I32)
+    for k in range(5):
+        irow_ref[:, k * 128 : (k + 1) * 128] = orow[pl.ds(k * 128, 128)].reshape(1, 128)
+    cyc_ref[0:20, :] = cyc_in[...]
+    cyc_ref[20:24, :] = jnp.zeros((4, 640), BF16)
+    cyc_ref[20:24, 0:64] = jnp.broadcast_to(prow[...].reshape(1, 64), (4, 64)).astype(BF16)
     diag = lax.broadcasted_iota(I32, (128, 128), 0) == lax.broadcasted_iota(I32, (128, 128), 1)
     for k in range(5):
         lab = jnp.broadcast_to(irow_ref[:, k * 128 : (k + 1) * 128], (128, 128))
@@ -81,12 +85,12 @@
 
     pl.semaphore_wait(bar, NZ * NR - 1 + NY - 1)
 
-    core = lax.rem(r, 2)
-    sends = lax.rem(z, 2) == core
+    side, core = lax.rem(lax.div(r, 2), 2), lax.rem(r, 2)
+    sends = lax.rem(z, 4) == lax.rem(r, 4)
 
     @pl.when(sends)
     def _():
-        to = cyc_g.at[y, core, lax.div(z, 2)]
+        to = cyc_g.at[side, core, lax.div(z, 4), y]
         local(cyc_ref, to, c_recv.at[0])
         for k in (4, 3, 5, 2, 6, 1, 7):
             remote(cyc_ref, to, c_send.at[0], c_recv.at[0], dev(z + k, y, r))
@@ -96,14 +100,21 @@
         remote(lad_hbm.at[rows], wbuf.at[1, rows], w_send, w_recv.at[1, h], dev(z + 1, y, r))
         remote(lad_hbm.at[rows], wbuf.at[3, rows], w_send, w_recv.at[3, h], dev(z - 1, y, r))
 
-    part = cyc_g.at[y, core]
+    part = cyc_g.at[side, core, :, y]
     await_bytes(part, c_recv.at[0])
     for k in (2, 1, 3):
         remote(part, part, c_send.at[1], c_recv.at[1], dev(z, y + k, r))
-    await_bytes(cyc_g.at[pl.ds(0, NY - 1), 0], c_recv.at[1])
-    part = cyc_g.at[:, core]
-    remote(part, part, c_send.at[2], c_recv.at[2], dev(z, y, r + 1 - 2 * core))
+    await_bytes(cyc_g.at[0, 0, :, pl.ds(0, NY - 1)], c_recv.at[1])
+    for h, dr in ((0, -2), (1, 2)):
+        part = cyc_g.at[side, core, h]
+        remote(part, part, c_send.at[2], c_recv.at[2], dev(z, y, r + dr))
+    partner = dev(z, y, r + 1 - 2 * core)
+    part = cyc_g.at[side, core]
+    remote(part, part, c_send.at[3], c_recv.at[3], partner)
+    part = cyc_g.at[1 - side, core]
     await_bytes(part, c_recv.at[2])
+    remote(part, part, c_send.at[3], c_recv.at[3], partner)
+    await_bytes(cyc_g.at[:, 0], c_recv.at[3])
 
     def forward(h):
         rows = pl.ds(h * 640, 640)
@@ -112,7 +123,7 @@
             remote(wbuf.at[a, rows], wbuf.at[b, rows], w_send, w_recv.at[b, h], dev(z + dz, y, r))
 
     for p in range(NZ * NY):
-        w_stage[p * 20 : p * 20 + 20, :] = cyc_g[p % NY, (p // NY) % 2, p // NY // 2][:20, :].astype(F32)
+        w_stage[p * 20 : p * 20 + 20, :] = cyc_g[p // NY % 4 // 2, p // NY % 2, p // NY // 4, p % NY][:20, :].astype(F32)
 
     def mask_w(c, _):
         rows = pl.ds(pl.multiple_of(c * 128, 128), 128)
@@ -128,22 +139,22 @@
         await_bytes(amp_v.at[pl.ds(0, 16)], amp_sem.at[b])
 
         def quad(q, _):
-            ij = b * 16 + q * 4
-            x = amp_v[pl.ds(ij, 4)].reshape(256, 640)
+            ij = b * 16 + q * 8
+            x = amp_v[pl.ds(ij, 8)].reshape(512, 640)
             v = jnp.dot(x, w_b[...], preferred_element_type=F32) + x.astype(F32)
-            for e in range(4):
+            for e in range(8):
                 label = pirr[ij + e]
-                at = pl.ds(pl.multiple_of((q * 4 + e) * 64, 64), 64)
+                at = pl.ds((q * 8 + e) * 65, 64)
                 for k in range(5):
                     cols = slice(k * 128, (k + 1) * 128)
                     y_stage[k, at, :] = jnp.where(irr_x[:, cols] == label, v[e * 64 : (e + 1) * 64, cols], 0.0)
             return 0
 
-        lax.fori_loop(0, 4, quad, 0)
+        lax.fori_loop(0, 2, quad, 0)
 
         def turn(c, _):
             at = pl.ds(pl.multiple_of(b * 16, 16), 16)
-            got = [y_stage[k, pl.ds(c * 8 + i, 16, stride=64), :].astype(BF16) for i in range(8) for k in range(5)]
+            got = [y_stage[k, pl.ds(c * 8 + i, 16, stride=65), :].astype(BF16) for i in range(8) for k in range(5)]
             for i in range(40):
                 dressed[c * 40 + i, at, :] = got[i]
             return 0
@@ -254,7 +265,7 @@
         multiply(x, wbuf.at[o + 2], ob)
         scatter(ob, rr, n, r_recv.at[item])
 
-    last = None
+    pending = []
     for i, delta in enumerate(WAY):
         if i + WINDOW < 8:
             sent(delta)
@@ -264,10 +275,11 @@
             continue
         for item in TODO[delta]:
             item_step(item)
-            if last is not None:
-                reduce(last)
-            last = item
-    reduce(last)
+            if pending and item < 7:
+                reduce(pending.pop(0))
+            pending.append(item)
+    for item in pending:
+        reduce(item)
 
     diag64 = lax.broadcasted_iota(I32, (64, 128), 0) == lax.broadcasted_iota(I32, (64, 128), 1)
     await_bytes(outb, f_recv)
@@ -279,7 +291,7 @@
             lab = lab + jnp.where(bb == k, irow_ref[:, k * 128 : (k + 1) * 128], 0)
         lab = jnp.bitwise_xor(lab, la).astype(F32)
         for yy in range(NY):
-            rowl = cyc_g[yy, core, lax.div(r, 2)][20:21, 0:128].astype(F32)
+            rowl = cyc_g[side, core, lax.div(r, 4), yy][20:21, 0:128].astype(F32)
             col = jnp.sum(jnp.where(diag64, jnp.broadcast_to(rowl, (64, 128)), 0.0), axis=1, keepdims=True)
             keep = jnp.broadcast_to(col, (64, 128)) == lab
             got = outb[yy * 64 : (yy + 1) * 64, j * 128 : (j + 1) * 128].astype(F32)
@@ -287,11 +299,12 @@
 
     @pl.when(sends)
     def _():
-        await_bytes(cyc_g.at[0, 0], c_send.at[0])
-        await_bytes(cyc_g.at[0, 1, pl.ds(0, 3)], c_send.at[0])
-
-    await_bytes(cyc_g.at[pl.ds(0, NY - 1), 0], c_send.at[1])
-    await_bytes(cyc_g.at[:, 0], c_send.at[2])
+        await_bytes(cyc_g.at[0, 0, 0], c_send.at[0])
+        await_bytes(cyc_g.at[0, 0, 0, pl.ds(0, 3)], c_send.at[0])
+
+    await_bytes(cyc_g.at[0, 0, :, pl.ds(0, NY - 1)], c_send.at[1])
+    await_bytes(cyc_g.at[0, 0], c_send.at[2])
+    await_bytes(cyc_g.at[:, 0], c_send.at[3])
     await_bytes(wbuf.at[pl.ds(0, 4)], w_send)
     for delta in WAY[8 - WINDOW :]:
         sent(delta)
@@ -308,11 +321,6 @@
 
 
 def shards(amplitudes, cycle_integrals, ladder_integrals, orbital_irrep, pair_irrep, tile_owners, ladder_tiles):
-    row = lax.broadcasted_iota(I32, (24, 640), 0)
-    cyc = jnp.where(row < 20, jnp.pad(cycle_integrals, ((0, 4), (0, 0))), jnp.zeros((), BF16))
-    labels = jnp.pad(pair_irrep, (0, 576))[None, :].astype(BF16)
-    cyc = jnp.where(row == 20, labels, cyc)
-    cyc = jnp.where(row == 21, orbital_irrep[None, :].astype(BF16), cyc)
     hbm = pl.BlockSpec(memory_space=pltpu.MemorySpace.HBM)
     vmem = pl.BlockSpec(memory_space=pltpu.MemorySpace.VMEM)
     smem = pl.BlockSpec(memory_space=pltpu.MemorySpace.SMEM)
@@ -320,17 +328,18 @@
     out = pl.pallas_call(
         kernel,
         out_shape=jax.ShapeDtypeStruct((256, 512), BF16),
-        in_specs=[hbm, vmem, hbm, smem, smem, smem, smem],
+        in_specs=[hbm, vmem, hbm, vmem, vmem, smem, smem, smem, smem],
         out_specs=vmem,
         scratch_shapes=[
             pltpu.VMEM((64, 64, 640), BF16),
-            pltpu.VMEM((4, 2, 4, 24, 640), BF16),
+            pltpu.VMEM((24, 640), BF16),
+            pltpu.VMEM((2, 2, 2, 4, 24, 640), BF16),
             pltpu.VMEM((640, 640), F32),
             pltpu.VMEM((640, 640), BF16),
             pltpu.VMEM((1, 640), I32),
             pltpu.VMEM((64, 640), I32),
             pltpu.VMEM((640, 128), I32),
-            pltpu.VMEM((5, 1024, 128), F32),
+            pltpu.VMEM((5, 1152, 128), F32),
             pltpu.VMEM((320, 64, 128), BF16),
             pltpu.VMEM((8, 4, 64, 1280), BF16),
             pltpu.VMEM((7, 256, 1280), BF16),
@@ -346,8 +355,8 @@
             pltpu.VMEM((256, 512), BF16),
             dma((4,)),
             dma,
-            dma((3,)),
-            dma((3,)),
+            dma((4,)),
+            dma((4,)),
             dma,
             dma((5, 2)),
             dma((8,)),
@@ -365,8 +374,10 @@
         name="ladder",
     )(
         amplitudes,
-        cyc,
+        cycle_integrals,
         ladder_integrals.reshape(1280, 512),
+        orbital_irrep,
+        pair_irrep,
         tile_owners,
         ladder_tiles.T,
         orbital_irrep,

time: 122 us -> 113 us (0.926)
  Pallas kernels: 117 us -> 111 us
  other arithmetic: 2.8 us -> 0 us
    pallas_call x1, Pallas kernels: 117 us -> 111 us  [shards(): pl.pallas_call(kernel, out_shape=jax.ShapeDtypeStruct((256, 512), BF16),...]
    select_n x1 -> x0, other arithmetic: 1.44 us -> none  [shards(): cyc = jnp.where(row == 21, orbital_irrep[None, :].astype(BF16), cyc)]
where the time goes in v3:
time: 113 us
  Pallas kernels  111 us (98%)
  local copies, waits for them, and re-layouts  1.67 us (1%)
    pallas_call x1, Pallas kernels, shards(): pl.pallas_call(kernel, out_shape=jax.ShapeDtypeStruct((256, 512), BF16),...  111 us

profile of v3, /device:TPU:4, one launch (start us, length us, event | category | flops | bytes accessed | tf_op | source)
XLA Modules:
  0.0 112.6 jit_solution(1579339422329770471)
XLA Ops:
  0.0 111.0 %ladder.1 = bf16[256,512]{1,0:T(8,128)(2,1)} custom-call(bf16[64,64,640]{2,1,0:T(8,128)(2,1)} %amp_hbm.1, bf16[20,640]{1,0:T(8,128)(2,1)} %cyc_in.1, bf16[1280,512]{1,0:T(8,128)(2,1)} %bitcast.3, s32[640]{0:T(1024)} %oirr.1, s32[64]{0:T(128)} %pirr.1, s32[8,320]{1,0:T(8,128)} %towners.1, s32[4,32]{1,0:T(4,128)} %bitcast.5, s32[640]{0:T(1024)} %oirr.1, s32[64]{0:T(128)} %pirr.1), custom_call_target="tpu_custom_call" | custom-call | tf_op jit(solution)/shard_map/ladder/pallas_call | solution.py:328
  111.0 1.7 %copy.9 = bf16[1,256,512]{2,1,0:T(8,128)(2,1)} copy(bf16[1,256,512]{2,1,0:T(8,128)(2,1)} %bitcast.4) | data formatting | bytes 524288

commit v4 on v3

--- a/solution.py
+++ b/solution.py
@@ -12,7 +12,7 @@
 WAY = (0, 3, -3, 4, 1, -1, 2, -2)
 NEAR = {0: 0, 1: 1, -1: 2, 2: 5, -2: 6}
 FAR = {3: 0, -3: 1, 4: 2}
-TODO = {0: (0,), 1: (1,), -1: (2,), 2: (3, 4, 5), -2: (6, 7, 8)}
+TODO = {0: (0,), 1: (1,), -1: (2,), 2: (3, 4, 5), -2: (6,)}
 WINDOW = 3
 
 
@@ -21,11 +21,12 @@
 
 
 def kernel(
-    amp_hbm, cyc_in, lad_hbm, orow, prow, towners, ltiles, oirr, pirr,
-    out_ref,
-    amp_v, cyc_ref, cyc_g, w_stage, w_b, irow_ref, irr_x, irr_c, y_stage, dressed, d_send,
+    amp_hbm, cyc_hbm, lad_hbm, to_hbm, lt_hbm, oi_hbm, pi_hbm,
+    out_hbm,
+    cyc_in, orow, prow, towners, ltiles, oirr, pirr, out_ref,
+    row_lab, col_lab, amp_v, cyc_ref, cyc_g, w_stage, w_b, irow_ref, irr_x, irr_c, y_stage, dressed, d_send,
     recv_f, recv_h, far, wbuf, ob_f, ob_h, rr_f, rr_h, fb_f, fb_h, outb,
-    amp_sem, own_sem, c_send, c_recv, w_send, w_recv, a_send, a_recv,
+    in_sem, out_sem, amp_sem, own_sem, c_send, c_recv, w_send, w_recv, a_send, a_recv,
     x_send, x_recv, r_send, r_recv, f_send, f_recv,
 ):
     pair = lax.axis_index("pair")
@@ -47,28 +48,46 @@
     def await_bytes(ref, sem):
         pltpu.make_async_copy(ref, ref, sem).wait()
 
+    bar = pltpu.get_barrier_semaphore()
+
+    def greet(where):
+        pl.semaphore_signal(bar, inc=1, device_id=where, device_id_type=pl.DeviceIdType.MESH)
+
+    for k in (1, 7, 2, 6, 3, 5, 4):
+        greet(dev(z + k, y, r))
+    for k in range(1, NR):
+        greet(dev(z, y, r + k))
+    for k in range(1, NY):
+        greet(dev(z, y + k, r))
+    offset = lax.rem(z + NZ - r, NZ)
+    for o, s in FULL[1:] + HALF:
+        greet(dev(z + o, y, z + s))
+    for k in range(1, NR):
+        greet(dev(r + jnp.where(offset == 3, 1, jnp.where(offset == 5, -1, jnp.where(offset == 4, 2, 0))), y, r + k))
+
+    @pl.when(offset != 0)
+    def _():
+        greet(dev(z, y, z))
+        greet(dev(r + jnp.where(offset == 3, 1, jnp.where(offset == 5, -1, jnp.where(offset == 4, 2, 0))), y, r))
+
+    @pl.when(offset == 4)
+    def _():
+        for k in range(NR):
+            greet(dev(r - 2, y, k))
+
+    small = (
+        (cyc_hbm, cyc_in), (oi_hbm, orow), (pi_hbm, prow), (to_hbm, towners),
+        (lt_hbm, ltiles), (oi_hbm, oirr), (pi_hbm, pirr),
+    )
+    for i, (src, dst) in enumerate(small):
+        local(src, dst, in_sem.at[i])
     for b in range(4):
         rows = pl.ds(b * 16, 16)
         local(amp_hbm.at[rows], amp_v.at[rows], amp_sem.at[b])
     local(lad_hbm, wbuf.at[2], own_sem)
 
-    bar = pltpu.get_barrier_semaphore()
-    me = z * NR + r
-
-    def greet(k, _):
-        i = lax.rem(me + k, NZ * NR)
-        pl.semaphore_signal(
-            bar, inc=1, device_id=dev(lax.div(i, NR), y, lax.rem(i, NR)),
-            device_id_type=pl.DeviceIdType.MESH,
-        )
-        return 0
-
-    lax.fori_loop(1, NZ * NR, greet, 0)
-    for k in range(1, NY):
-        pl.semaphore_signal(
-            bar, inc=1, device_id=dev(z, y + k, r),
-            device_id_type=pl.DeviceIdType.MESH,
-        )
+    for i, (src, dst) in enumerate(small):
+        pltpu.make_async_copy(src, dst, in_sem.at[i]).wait()
     for k in range(5):
         irow_ref[:, k * 128 : (k + 1) * 128] = orow[pl.ds(k * 128, 128)].reshape(1, 128)
     cyc_ref[0:20, :] = cyc_in[...]
@@ -83,7 +102,7 @@
     for k in range(5):
         irr_x[:, k * 128 : (k + 1) * 128] = jnp.bitwise_xor(slab, irow_ref[:, k * 128 : (k + 1) * 128])
 
-    pl.semaphore_wait(bar, NZ * NR - 1 + NY - 1)
+    pl.semaphore_wait(bar, 34 + jnp.where(offset == 4, 8, 0) - jnp.where(offset == 0, 2, 0))
 
     side, core = lax.rem(lax.div(r, 2), 2), lax.rem(r, 2)
     sends = lax.rem(z, 4) == lax.rem(r, 4)
@@ -196,14 +215,30 @@
         at = FAR[delta]
         await_bytes(far.at[at], x_recv.at[at])
         if delta == 4:
-            remote(far.at[at, pl.ds(0, 128)], recv_h.at[0], x_send, a_recv.at[7], dev(z + 2, y, r))
-            remote(far.at[at, pl.ds(128, 128)], recv_h.at[1], x_send, a_recv.at[8], dev(z - 2, y, r))
+            for part in range(2):
+                rows = pl.ds(part * 64, 64)
+                remote(far.at[at, rows], recv_h.at[0, rows], x_send, a_recv.at[7 + part], dev(z + 2, y, r))
+                low = pl.ds(128 + part * 64, 64)
+                remote(far.at[at, low], recv_h.at[1, rows], x_send, a_recv.at[9 + part], dev(z - 2, y, r))
         else:
             remote(far.at[at], recv_f.at[3 + at], x_send, a_recv.at[3 + at], dev(z + 1 - 2 * at, y, r))
 
     for delta in WAY[:WINDOW]:
         send(delta)
     forward(1)
+
+    diag64 = lax.broadcasted_iota(I32, (64, 128), 0) == lax.broadcasted_iota(I32, (64, 128), 1)
+    for yy in range(NY):
+        rowl = cyc_g[side, core, lax.div(r, 4), yy][20:21, 0:128].astype(F32)
+        col = jnp.sum(jnp.where(diag64, jnp.broadcast_to(rowl, (64, 128)), 0.0), axis=1, keepdims=True)
+        row_lab[yy * 64 : (yy + 1) * 64, :] = jnp.broadcast_to(col, (64, 128))
+    for j in range(4):
+        t = ltiles[j, pair]
+        la, bb = oirr[lax.div(t, 5)], lax.rem(t, 5)
+        lab = jnp.zeros((1, 128), I32)
+        for k in range(5):
+            lab = lab + jnp.where(bb == k, irow_ref[:, k * 128 : (k + 1) * 128], 0)
+        col_lab[j : j + 1, :] = jnp.bitwise_xor(lab, la).astype(F32)
 
     def multiply(x, w, o):
         def cols(n, _):
@@ -250,11 +285,29 @@
 
     ready = {2}
 
+    def half_step(item, part):
+        h, rows = item - 7, pl.ds(part * 64, 64)
+        await_bytes(recv_h.at[h, rows], a_recv.at[7 + 2 * h + part])
+        multiply(recv_h.at[h, rows], wbuf.at[HALF[h][0] + 2], ob_h.at[h, rows])
+
+        def piece(q):
+            return ob_h.at[h, pl.ds(pl.multiple_of(q * 16, 16), 16)]
+
+        for k in (2, 1, 3):
+            q = part * 4 + lax.rem(r + k, 4)
+            remote(piece(q), rr_h.at[h, r], r_send, r_recv.at[item], dev(z, y, q))
+        q = part * 4 + lax.rem(r, 4)
+
+        @pl.when(q == r)
+        def _():
+            local(piece(r), rr_h.at[h, r], r_recv.at[item])
+
+        @pl.when(q != r)
+        def _():
+            remote(piece(q), rr_h.at[h, r], r_send, r_recv.at[item], dev(z, y, q))
+
     def item_step(item):
-        if item < 7:
-            o, x, ob, rr, n = FULL[item][0], recv_f.at[item], ob_f.at[item], rr_f.at[item], 32
-        else:
-            o, x, ob, rr, n = HALF[item - 7][0], recv_h.at[item - 7], ob_h.at[item - 7], rr_h.at[item - 7], 16
+        o, x, ob, rr, n = FULL[item][0], recv_f.at[item], ob_f.at[item], rr_f.at[item], 32
         if item == 0:
             await_bytes(wbuf.at[2], own_sem)
         if o in (2, -2) and o + 2 not in ready:
@@ -275,27 +328,22 @@
             continue
         for item in TODO[delta]:
             item_step(item)
-            if pending and item < 7:
+            if len(pending) > 1:
                 reduce(pending.pop(0))
             pending.append(item)
-    for item in pending:
+    for part in range(2):
+        for item in (7, 8):
+            half_step(item, part)
+    for item in (*pending, 7, 8):
         reduce(item)
 
-    diag64 = lax.broadcasted_iota(I32, (64, 128), 0) == lax.broadcasted_iota(I32, (64, 128), 1)
     await_bytes(outb, f_recv)
-    for j in range(4):
-        t = ltiles[j, pair]
-        la, bb = oirr[lax.div(t, 5)], lax.rem(t, 5)
-        lab = jnp.zeros((1, 128), I32)
-        for k in range(5):
-            lab = lab + jnp.where(bb == k, irow_ref[:, k * 128 : (k + 1) * 128], 0)
-        lab = jnp.bitwise_xor(lab, la).astype(F32)
-        for yy in range(NY):
-            rowl = cyc_g[side, core, lax.div(r, 4), yy][20:21, 0:128].astype(F32)
-            col = jnp.sum(jnp.where(diag64, jnp.broadcast_to(rowl, (64, 128)), 0.0), axis=1, keepdims=True)
-            keep = jnp.broadcast_to(col, (64, 128)) == lab
+    for yy in range(NY):
+        for j in range(4):
             got = outb[yy * 64 : (yy + 1) * 64, j * 128 : (j + 1) * 128].astype(F32)
+            keep = row_lab[yy * 64 : (yy + 1) * 64, :] == col_lab[j : j + 1, :]
             out_ref[yy * 64 : (yy + 1) * 64, j * 128 : (j + 1) * 128] = jnp.where(keep, got, 0.0).astype(BF16)
+    local(out_ref, out_hbm, out_sem)
 
     @pl.when(sends)
     def _():
@@ -318,19 +366,28 @@
 
     await_bytes(fb_f.at[pl.ds(0, 6)], f_send.at[1])
     await_bytes(fb_h, f_send.at[1])
+    pltpu.make_async_copy(out_ref, out_hbm, out_sem).wait()
 
 
 def shards(amplitudes, cycle_integrals, ladder_integrals, orbital_irrep, pair_irrep, tile_owners, ladder_tiles):
     hbm = pl.BlockSpec(memory_space=pltpu.MemorySpace.HBM)
-    vmem = pl.BlockSpec(memory_space=pltpu.MemorySpace.VMEM)
-    smem = pl.BlockSpec(memory_space=pltpu.MemorySpace.SMEM)
     dma = pltpu.SemaphoreType.DMA
     out = pl.pallas_call(
         kernel,
         out_shape=jax.ShapeDtypeStruct((256, 512), BF16),
-        in_specs=[hbm, vmem, hbm, vmem, vmem, smem, smem, smem, smem],
-        out_specs=vmem,
+        in_specs=[hbm] * 7,
+        out_specs=hbm,
         scratch_shapes=[
+            pltpu.VMEM((20, 640), BF16),
+            pltpu.VMEM((640,), I32),
+            pltpu.VMEM((64,), I32),
+            pltpu.SMEM((8, 320), I32),
+            pltpu.SMEM((4, 32), I32),
+            pltpu.SMEM((640,), I32),
+            pltpu.SMEM((64,), I32),
+            pltpu.VMEM((256, 512), BF16),
+            pltpu.VMEM((256, 128), F32),
+            pltpu.VMEM((4, 128), F32),
             pltpu.VMEM((64, 64, 640), BF16),
             pltpu.VMEM((24, 640), BF16),
             pltpu.VMEM((2, 2, 2, 4, 24, 640), BF16),
@@ -353,6 +410,8 @@
             pltpu.VMEM((7, 32, 512), BF16),
             pltpu.VMEM((2, 16, 512), BF16),
             pltpu.VMEM((256, 512), BF16),
+            dma((7,)),
+            dma,
             dma((4,)),
             dma,
             dma((4,)),
@@ -360,7 +419,7 @@
             dma,
             dma((5, 2)),
             dma((8,)),
-            dma((9,)),
+            dma((11,)),
             dma,
             dma((3,)),
             dma,
@@ -376,8 +435,6 @@
         amplitudes,
         cycle_integrals,
         ladder_integrals.reshape(1280, 512),
-        orbital_irrep,
-        pair_irrep,
         tile_owners,
         ladder_tiles.T,
         orbital_irrep,

time: 113 us -> 109 us (0.965)
  Pallas kernels: 111 us -> 107 us
    pallas_call x1, Pallas kernels: 111 us -> 107 us  [shards(): pl.pallas_call(kernel, out_shape=jax.ShapeDtypeStruct((256, 512), BF16),...]
where the time goes in v4:
time: 109 us
  Pallas kernels  107 us (98%)
  local copies, waits for them, and re-layouts  1.67 us (2%)
    pallas_call x1, Pallas kernels, shards(): pl.pallas_call(kernel, out_shape=jax.ShapeDtypeStruct((256, 512), BF16),...  107 us

profile of v4, /device:TPU:4, one launch (start us, length us, event | category | flops | bytes accessed | tf_op | source)
XLA Modules:
  0.0 108.6 jit_solution(4120784491005874518)
XLA Ops:
  0.0 106.9 %ladder.1 = bf16[256,512]{1,0:T(8,128)(2,1)} custom-call(bf16[64,64,640]{2,1,0:T(8,128)(2,1)} %amp_hbm.1, bf16[20,640]{1,0:T(8,128)(2,1)} %cyc_hbm.1, bf16[1280,512]{1,0:T(8,128)(2,1)} %bitcast.3, s32[8,320]{1,0:T(8,128)} %to_hbm.1, s32[4,32]{1,0:T(4,128)} %bitcast.5, s32[640]{0:T(1024)} %oi_hbm.1, s32[64]{0:T(128)} %pi_hbm.1), custom_call_target="tpu_custom_call" | custom-call | tf_op jit(solution)/shard_map/ladder/pallas_call | solution.py:375
  106.9 1.7 %copy.9 = bf16[1,256,512]{2,1,0:T(8,128)(2,1)} copy(bf16[1,256,512]{2,1,0:T(8,128)(2,1)} %bitcast.4) | data formatting | bytes 524288

commit v5 on v4

--- a/solution.py
+++ b/solution.py
@@ -22,10 +22,10 @@
 
 def kernel(
     amp_hbm, cyc_hbm, lad_hbm, to_hbm, lt_hbm, oi_hbm, pi_hbm,
-    out_hbm,
-    cyc_in, orow, prow, towners, ltiles, oirr, pirr, out_ref,
-    row_lab, col_lab, amp_v, cyc_ref, cyc_g, w_stage, w_b, irow_ref, irr_x, irr_c, y_stage, dressed, d_send,
-    recv_f, recv_h, far, wbuf, ob_f, ob_h, rr_f, rr_h, fb_f, fb_h, outb,
+    out_hbm, keep_hbm,
+    cyc_in, orow, prow, towners, ltiles, oirr, pirr, keep,
+    amp_v, cyc_ref, cyc_g, w_stage, w_b, irow_ref, irr_x, irr_c, y_stage, dressed, d_send,
+    recv_f, recv_h, far, wbuf, ob_f, ob_h, rr_f, rr_h, fb_f, fb_h,
     in_sem, out_sem, amp_sem, own_sem, c_send, c_recv, w_send, w_recv, a_send, a_recv,
     x_send, x_recv, r_send, r_recv, f_send, f_recv,
 ):
@@ -59,22 +59,6 @@
         greet(dev(z, y, r + k))
     for k in range(1, NY):
         greet(dev(z, y + k, r))
-    offset = lax.rem(z + NZ - r, NZ)
-    for o, s in FULL[1:] + HALF:
-        greet(dev(z + o, y, z + s))
-    for k in range(1, NR):
-        greet(dev(r + jnp.where(offset == 3, 1, jnp.where(offset == 5, -1, jnp.where(offset == 4, 2, 0))), y, r + k))
-
-    @pl.when(offset != 0)
-    def _():
-        greet(dev(z, y, z))
-        greet(dev(r + jnp.where(offset == 3, 1, jnp.where(offset == 5, -1, jnp.where(offset == 4, 2, 0))), y, r))
-
-    @pl.when(offset == 4)
-    def _():
-        for k in range(NR):
-            greet(dev(r - 2, y, k))
-
     small = (
         (cyc_hbm, cyc_in), (oi_hbm, orow), (pi_hbm, prow), (to_hbm, towners),
         (lt_hbm, ltiles), (oi_hbm, oirr), (pi_hbm, pirr),
@@ -102,7 +86,7 @@
     for k in range(5):
         irr_x[:, k * 128 : (k + 1) * 128] = jnp.bitwise_xor(slab, irow_ref[:, k * 128 : (k + 1) * 128])
 
-    pl.semaphore_wait(bar, 34 + jnp.where(offset == 4, 8, 0) - jnp.where(offset == 0, 2, 0))
+    pl.semaphore_wait(bar, 2 * (NZ - 1) + NY - 1)
 
     side, core = lax.rem(lax.div(r, 2), 2), lax.rem(r, 2)
     sends = lax.rem(z, 4) == lax.rem(r, 4)
@@ -228,17 +212,19 @@
     forward(1)
 
     diag64 = lax.broadcasted_iota(I32, (64, 128), 0) == lax.broadcasted_iota(I32, (64, 128), 1)
-    for yy in range(NY):
-        rowl = cyc_g[side, core, lax.div(r, 4), yy][20:21, 0:128].astype(F32)
-        col = jnp.sum(jnp.where(diag64, jnp.broadcast_to(rowl, (64, 128)), 0.0), axis=1, keepdims=True)
-        row_lab[yy * 64 : (yy + 1) * 64, :] = jnp.broadcast_to(col, (64, 128))
     for j in range(4):
         t = ltiles[j, pair]
         la, bb = oirr[lax.div(t, 5)], lax.rem(t, 5)
         lab = jnp.zeros((1, 128), I32)
         for k in range(5):
             lab = lab + jnp.where(bb == k, irow_ref[:, k * 128 : (k + 1) * 128], 0)
-        col_lab[j : j + 1, :] = jnp.bitwise_xor(lab, la).astype(F32)
+        lab = jnp.bitwise_xor(lab, la).astype(F32)
+        for yy in range(NY):
+            rowl = cyc_g[side, core, lax.div(r, 4), yy][20:21, 0:128].astype(F32)
+            col = jnp.sum(jnp.where(diag64, jnp.broadcast_to(rowl, (64, 128)), 0.0), axis=1, keepdims=True)
+            same = jnp.broadcast_to(col, (64, 128)) == lab
+            keep[yy * 64 : (yy + 1) * 64, j * 128 : (j + 1) * 128] = jnp.where(same, 1.0, 0.0).astype(BF16)
+    local(keep, keep_hbm, out_sem)
 
     def multiply(x, w, o):
         def cols(n, _):
@@ -269,7 +255,7 @@
         for q in range(1, NR):
             total = total + rr[q].astype(F32)
         fb[...] = total.astype(BF16)
-        rows = outb.at[pl.ds(pl.multiple_of(row, 16), n)]
+        rows = out_hbm.at[pl.ds(pl.multiple_of(row, 16), n)]
         level = wrap(z + s, NZ)
         if item == 0:
 
@@ -337,13 +323,7 @@
     for item in (*pending, 7, 8):
         reduce(item)
 
-    await_bytes(outb, f_recv)
-    for yy in range(NY):
-        for j in range(4):
-            got = outb[yy * 64 : (yy + 1) * 64, j * 128 : (j + 1) * 128].astype(F32)
-            keep = row_lab[yy * 64 : (yy + 1) * 64, :] == col_lab[j : j + 1, :]
-            out_ref[yy * 64 : (yy + 1) * 64, j * 128 : (j + 1) * 128] = jnp.where(keep, got, 0.0).astype(BF16)
-    local(out_ref, out_hbm, out_sem)
+    await_bytes(out_hbm, f_recv)
 
     @pl.when(sends)
     def _():
@@ -366,17 +346,17 @@
 
     await_bytes(fb_f.at[pl.ds(0, 6)], f_send.at[1])
     await_bytes(fb_h, f_send.at[1])
-    pltpu.make_async_copy(out_ref, out_hbm, out_sem).wait()
+    pltpu.make_async_copy(keep, keep_hbm, out_sem).wait()
 
 
 def shards(amplitudes, cycle_integrals, ladder_integrals, orbital_irrep, pair_irrep, tile_owners, ladder_tiles):
     hbm = pl.BlockSpec(memory_space=pltpu.MemorySpace.HBM)
     dma = pltpu.SemaphoreType.DMA
-    out = pl.pallas_call(
+    out, keep = pl.pallas_call(
         kernel,
-        out_shape=jax.ShapeDtypeStruct((256, 512), BF16),
+        out_shape=[pltpu.VMEM((256, 512), BF16)] * 2,
         in_specs=[hbm] * 7,
-        out_specs=hbm,
+        out_specs=[pl.BlockSpec(memory_space=pltpu.MemorySpace.VMEM)] * 2,
         scratch_shapes=[
             pltpu.VMEM((20, 640), BF16),
             pltpu.VMEM((640,), I32),
@@ -386,8 +366,6 @@
             pltpu.SMEM((640,), I32),
             pltpu.SMEM((64,), I32),
             pltpu.VMEM((256, 512), BF16),
-            pltpu.VMEM((256, 128), F32),
-            pltpu.VMEM((4, 128), F32),
             pltpu.VMEM((64, 64, 640), BF16),
             pltpu.VMEM((24, 640), BF16),
             pltpu.VMEM((2, 2, 2, 4, 24, 640), BF16),
@@ -409,7 +387,6 @@
             pltpu.VMEM((2, 8, 16, 512), BF16),
             pltpu.VMEM((7, 32, 512), BF16),
             pltpu.VMEM((2, 16, 512), BF16),
-            pltpu.VMEM((256, 512), BF16),
             dma((7,)),
             dma,
             dma((4,)),
@@ -440,7 +417,7 @@
         orbital_irrep,
         pair_irrep,
     )
-    return out[None]
+    return jnp.where(keep != 0, out, jnp.zeros((), BF16))[None]
 
 
 def solution(mesh):

time: 109 us -> 106 us (0.972)
  local copies, waits for them, and re-layouts: 1.67 us -> 0 us
    unnamed x1 -> x0, local copies, waits for them, and re-layouts: 1.67 us -> none
    pallas_call x1, Pallas kernels: 107 us -> 106 us  [shards(): pl.pallas_call(kernel, out_shape=[pltpu.VMEM((256, 512), BF16)] * 2, in_s...]
where the time goes in v5:
time: 106 us
  Pallas kernels  106 us (100%)
    pallas_call x1, Pallas kernels, shards(): pl.pallas_call(kernel, out_shape=[pltpu.VMEM((256, 512), BF16)] * 2, in_s...  106 us

profile of v5, /device:TPU:4, one launch (start us, length us, event | category | flops | bytes accessed | tf_op | source)
XLA Modules:
  0.0 106.3 jit_solution(1798180074590939775)
XLA Ops:
  0.0 105.6 %ladder.1 = (bf16[256,512]{1,0:T(8,128)(2,1)S(1)}, bf16[256,512]{1,0:T(8,128)(2,1)S(1)}) custom-call(bf16[64,64,640]{2,1,0:T(8,128)(2,1)} %amp_hbm.1, bf16[20,640]{1,0:T(8,128)(2,1)} %cyc_hbm.1, bf16[1280,512]{1,0:T(8,128)(2,1)} %bitcast.4, s32[8,320]{1,0:T(8,128)} %to_hbm.1, s32[4,32]{1,0:T(4,128)} %bitcast.5, s32[640]{0:T(1024)} %oi_hbm.1, s32[64]{0:T(128)} %pi_hbm.1), custom_call_target="tpu_custom_call" | custom-call | tf_op jit(solution)/shard_map/ladder/pallas_call | solution.py:355
  105.6 0.7 fusion

commit v6 on v5

--- a/solution.py
+++ b/solution.py
@@ -65,11 +65,6 @@
     )
     for i, (src, dst) in enumerate(small):
         local(src, dst, in_sem.at[i])
-    for b in range(4):
-        rows = pl.ds(b * 16, 16)
-        local(amp_hbm.at[rows], amp_v.at[rows], amp_sem.at[b])
-    local(lad_hbm, wbuf.at[2], own_sem)
-
     for i, (src, dst) in enumerate(small):
         pltpu.make_async_copy(src, dst, in_sem.at[i]).wait()
     for k in range(5):
@@ -77,6 +72,28 @@
     cyc_ref[0:20, :] = cyc_in[...]
     cyc_ref[20:24, :] = jnp.zeros((4, 640), BF16)
     cyc_ref[20:24, 0:64] = jnp.broadcast_to(prow[...].reshape(1, 64), (4, 64)).astype(BF16)
+    pl.semaphore_wait(bar, 2 * (NZ - 1) + NY - 1)
+
+    side, core = lax.div(r, 2), lax.rem(r, 2)
+    sends = z == r
+
+    @pl.when(sends)
+    def _():
+        to = cyc_g.at[side, core, y]
+        local(cyc_ref, to, c_recv.at[0])
+        for k in (4, 3, 5, 2, 6, 1, 7):
+            remote(cyc_ref, to, c_send.at[0], c_recv.at[0], dev(z + k, y, r))
+
+    for h in range(2):
+        rows = pl.ds(h * 640, 640)
+        remote(lad_hbm.at[rows], wbuf.at[1, rows], w_send, w_recv.at[1, h], dev(z + 1, y, r))
+        remote(lad_hbm.at[rows], wbuf.at[3, rows], w_send, w_recv.at[3, h], dev(z - 1, y, r))
+
+    for b in range(4):
+        rows = pl.ds(b * 16, 16)
+        local(amp_hbm.at[rows], amp_v.at[rows], amp_sem.at[b])
+    local(lad_hbm, wbuf.at[2], own_sem)
+
     diag = lax.broadcasted_iota(I32, (128, 128), 0) == lax.broadcasted_iota(I32, (128, 128), 1)
     for k in range(5):
         lab = jnp.broadcast_to(irow_ref[:, k * 128 : (k + 1) * 128], (128, 128))
@@ -86,37 +103,20 @@
     for k in range(5):
         irr_x[:, k * 128 : (k + 1) * 128] = jnp.bitwise_xor(slab, irow_ref[:, k * 128 : (k + 1) * 128])
 
-    pl.semaphore_wait(bar, 2 * (NZ - 1) + NY - 1)
-
-    side, core = lax.rem(lax.div(r, 2), 2), lax.rem(r, 2)
-    sends = lax.rem(z, 4) == lax.rem(r, 4)
-
-    @pl.when(sends)
-    def _():
-        to = cyc_g.at[side, core, lax.div(z, 4), y]
-        local(cyc_ref, to, c_recv.at[0])
-        for k in (4, 3, 5, 2, 6, 1, 7):
-            remote(cyc_ref, to, c_send.at[0], c_recv.at[0], dev(z + k, y, r))
-
-    for h in range(2):
-        rows = pl.ds(h * 640, 640)
-        remote(lad_hbm.at[rows], wbuf.at[1, rows], w_send, w_recv.at[1, h], dev(z + 1, y, r))
-        remote(lad_hbm.at[rows], wbuf.at[3, rows], w_send, w_recv.at[3, h], dev(z - 1, y, r))
-
-    part = cyc_g.at[side, core, :, y]
+    part = cyc_g.at[side, core, y]
     await_bytes(part, c_recv.at[0])
     for k in (2, 1, 3):
         remote(part, part, c_send.at[1], c_recv.at[1], dev(z, y + k, r))
-    await_bytes(cyc_g.at[0, 0, :, pl.ds(0, NY - 1)], c_recv.at[1])
-    for h, dr in ((0, -2), (1, 2)):
-        part = cyc_g.at[side, core, h]
-        remote(part, part, c_send.at[2], c_recv.at[2], dev(z, y, r + dr))
+    await_bytes(cyc_g.at[0, 0, pl.ds(0, NY - 1)], c_recv.at[1])
+    part = cyc_g.at[side, core]
+    for k in (2, 1, 3):
+        remote(part, part, c_send.at[2], c_recv.at[2], dev(z, y, r + 2 * k))
     partner = dev(z, y, r + 1 - 2 * core)
-    part = cyc_g.at[side, core]
     remote(part, part, c_send.at[3], c_recv.at[3], partner)
-    part = cyc_g.at[1 - side, core]
-    await_bytes(part, c_recv.at[2])
-    remote(part, part, c_send.at[3], c_recv.at[3], partner)
+    await_bytes(cyc_g.at[pl.ds(0, 3), 0], c_recv.at[2])
+    for k in range(1, 4):
+        part = cyc_g.at[lax.rem(side + k, 4), core]
+        remote(part, part, c_send.at[3], c_recv.at[3], partner)
     await_bytes(cyc_g.at[:, 0], c_recv.at[3])
 
     def forward(h):
@@ -126,7 +126,7 @@
             remote(wbuf.at[a, rows], wbuf.at[b, rows], w_send, w_recv.at[b, h], dev(z + dz, y, r))
 
     for p in range(NZ * NY):
-        w_stage[p * 20 : p * 20 + 20, :] = cyc_g[p // NY % 4 // 2, p // NY % 2, p // NY // 4, p % NY][:20, :].astype(F32)
+        w_stage[p * 20 : p * 20 + 20, :] = cyc_g[p // NY // 2, p // NY % 2, p % NY][:20, :].astype(F32)
 
     def mask_w(c, _):
         rows = pl.ds(pl.multiple_of(c * 128, 128), 128)
@@ -220,7 +220,7 @@
             lab = lab + jnp.where(bb == k, irow_ref[:, k * 128 : (k + 1) * 128], 0)
         lab = jnp.bitwise_xor(lab, la).astype(F32)
         for yy in range(NY):
-            rowl = cyc_g[side, core, lax.div(r, 4), yy][20:21, 0:128].astype(F32)
+            rowl = cyc_g[side, core, yy][20:21, 0:128].astype(F32)
             col = jnp.sum(jnp.where(diag64, jnp.broadcast_to(rowl, (64, 128)), 0.0), axis=1, keepdims=True)
             same = jnp.broadcast_to(col, (64, 128)) == lab
             keep[yy * 64 : (yy + 1) * 64, j * 128 : (j + 1) * 128] = jnp.where(same, 1.0, 0.0).astype(BF16)
@@ -327,11 +327,11 @@
 
     @pl.when(sends)
     def _():
-        await_bytes(cyc_g.at[0, 0, 0], c_send.at[0])
-        await_bytes(cyc_g.at[0, 0, 0, pl.ds(0, 3)], c_send.at[0])
-
-    await_bytes(cyc_g.at[0, 0, :, pl.ds(0, NY - 1)], c_send.at[1])
-    await_bytes(cyc_g.at[0, 0], c_send.at[2])
+        await_bytes(cyc_g.at[0, 0], c_send.at[0])
+        await_bytes(cyc_g.at[0, 1, pl.ds(0, 3)], c_send.at[0])
+
+    await_bytes(cyc_g.at[0, 0, pl.ds(0, NY - 1)], c_send.at[1])
+    await_bytes(cyc_g.at[pl.ds(0, 3), 0], c_send.at[2])
     await_bytes(cyc_g.at[:, 0], c_send.at[3])
     await_bytes(wbuf.at[pl.ds(0, 4)], w_send)
     for delta in WAY[8 - WINDOW :]:
@@ -368,7 +368,7 @@
             pltpu.VMEM((256, 512), BF16),
             pltpu.VMEM((64, 64, 640), BF16),
             pltpu.VMEM((24, 640), BF16),
-            pltpu.VMEM((2, 2, 2, 4, 24, 640), BF16),
+            pltpu.VMEM((4, 2, 4, 24, 640), BF16),
             pltpu.VMEM((640, 640), F32),
             pltpu.VMEM((640, 640), BF16),
             pltpu.VMEM((1, 640), I32),

time: 106 us -> 106 us (level)
  no operation moved by 1% of the time
where the time goes in v6:
time: 106 us
  Pallas kernels  105 us (99%)
    pallas_call x1, Pallas kernels, shards(): pl.pallas_call(kernel, out_shape=[pltpu.VMEM((256, 512), BF16)] * 2, in_s...  105 us

profile of v6, /device:TPU:4, one launch (start us, length us, event | category | flops | bytes accessed | tf_op | source)
XLA Modules:
  0.0 105.9 jit_solution(5269357712264065534)
XLA Ops:
  0.0 105.2 %ladder.1 = (bf16[256,512]{1,0:T(8,128)(2,1)S(1)}, bf16[256,512]{1,0:T(8,128)(2,1)S(1)}) custom-call(bf16[64,64,640]{2,1,0:T(8,128)(2,1)} %amp_hbm.1, bf16[20,640]{1,0:T(8,128)(2,1)} %cyc_hbm.1, bf16[1280,512]{1,0:T(8,128)(2,1)} %bitcast.4, s32[8,320]{1,0:T(8,128)} %to_hbm.1, s32[4,32]{1,0:T(4,128)} %bitcast.5, s32[640]{0:T(1024)} %oi_hbm.1, s32[64]{0:T(128)} %pi_hbm.1), custom_call_target="tpu_custom_call" | custom-call | tf_op jit(solution)/shard_map/ladder/pallas_call | solution.py:355
  105.2 0.7 fusion

commit v7 on v6

--- a/solution.py
+++ b/solution.py
@@ -13,7 +13,7 @@
 NEAR = {0: 0, 1: 1, -1: 2, 2: 5, -2: 6}
 FAR = {3: 0, -3: 1, 4: 2}
 TODO = {0: (0,), 1: (1,), -1: (2,), 2: (3, 4, 5), -2: (6,)}
-WINDOW = 3
+WINDOW = 4
 
 
 def wrap(v, n):

time: 106 us -> 106 us (level)
  no operation moved by 1% of the time
where the time goes in v7:
time: 106 us
  Pallas kernels  105 us (99%)
    pallas_call x1, Pallas kernels, shards(): pl.pallas_call(kernel, out_shape=[pltpu.VMEM((256, 512), BF16)] * 2, in_s...  105 us

profile of v7, /device:TPU:4, one launch (start us, length us, event | category | flops | bytes accessed | tf_op | source)
XLA Modules:
  0.0 105.9 jit_solution(12074154909473810630)
XLA Ops:
  0.0 105.2 %ladder.1 = (bf16[256,512]{1,0:T(8,128)(2,1)S(1)}, bf16[256,512]{1,0:T(8,128)(2,1)S(1)}) custom-call(bf16[64,64,640]{2,1,0:T(8,128)(2,1)} %amp_hbm.1, bf16[20,640]{1,0:T(8,128)(2,1)} %cyc_hbm.1, bf16[1280,512]{1,0:T(8,128)(2,1)} %bitcast.4, s32[8,320]{1,0:T(8,128)} %to_hbm.1, s32[4,32]{1,0:T(4,128)} %bitcast.5, s32[640]{0:T(1024)} %oi_hbm.1, s32[64]{0:T(128)} %pi_hbm.1), custom_call_target="tpu_custom_call" | custom-call | tf_op jit(solution)/shard_map/ladder/pallas_call | solution.py:355
  105.2 0.7 fusion
